TPU v7x, 256 devices: a whole 4x4x8 slice. The times are simulated.
256 devices in a mesh: ab: 16 (over z_lo, y, core), cd: 16 (over z_hi, x).
Axes of the slice: x: 4, y: 4, z: 8 (z_hi: 4, z_lo: 2; z = z_hi * 2 + z_lo), core: 2. Of those that a mesh axis runs over, the one named last changes fastest.
Arguments:
- pair_values: bfloat16 [32768, 32768], P('ab', 'cd'), may hold values from -0.046875 to 0.046875
- amplitudes: bfloat16 [64, 800, 800], P('ab', 'cd'), may hold values from -6 to 6
- cd_first: int32 [32768], P('cd'), may hold values from 0 to 799, as said below
- cd_second: int32 [32768], P('cd'), may hold values from 0 to 799, as said below
- live_cols: int32 [16], P('cd'), may hold values from 512 to 2048, as said below
Outputs:
- ladder: bfloat16 [64, 32768], P(None, ('ab', 'cd'))
Inputs may be any that keep to these rules, and one draw needn't show every extreme that they name: `cd_first`: slot n lies in slab s = n // 2048 and its c lies in orbitals s * 50 to (s + 1) * 50 - 1. cd_second[n] >= cd_first[n] for every slot. `live_cols`: slots 0 and 1 of every slab are live.
All inputs are finite; a program needn't handle non-finite values.
Results may differ from a plain program's by a relative error of at most 0.0051.
Values may be sent and summed in bfloat16 or wider, within the bound.
A program may use at most 64 MiB of HBM per device.

v0:
```python
import jax
import jax.numpy as jnp
from jax import lax
from jax.sharding import PartitionSpec as P


def on_device(pair_values, amplitudes, cd_first, cd_second, live_cols):
    slab = lax.axis_index("cd")
    pair_block = amplitudes.shape[0]
    orbit_block = amplitudes.shape[1]
    orbitals = amplitudes.shape[2]
    columns = cd_first.shape[0]
    local_first = cd_first - slab * orbit_block
    own_flat = amplitudes.reshape(pair_block, orbit_block * orbitals)
    direct = jnp.take(own_flat, local_first * orbitals + cd_second, axis=1)
    whole = lax.all_gather(amplitudes, "cd", axis=1, tiled=True)
    whole_flat = whole.reshape(pair_block, orbitals * orbitals)
    crossed = jnp.take(whole_flat, cd_second * orbitals + cd_first, axis=1)
    live_count = live_cols[0]
    slots = jnp.arange(columns, dtype=jnp.int32)
    live = (slots < live_count).astype(jnp.float32)
    half = jnp.where(cd_first == cd_second, jnp.float32(0.5), jnp.float32(1.0))
    weight = half * live
    packed = ((direct.astype(jnp.float32) + crossed.astype(jnp.float32)) * weight[None, :]).astype(
        jnp.bfloat16
    )
    contract = (((1,), (1,)), ((), ()))
    partial_sums = lax.dot_general(
        lax.all_gather(packed, "ab", axis=0, tiled=True),
        pair_values,
        contract,
        preferred_element_type=jnp.float32,
    )
    return lax.psum_scatter(partial_sums, "cd", scatter_dimension=1, tiled=True).astype(
        jnp.bfloat16
    )


def solution(mesh):
    placed = (P("ab", "cd"), P("ab", "cd", None), P("cd"), P("cd"), P("cd"))
    return jax.shard_map(
        on_device, mesh=mesh, in_specs=placed, out_specs=P(None, ("ab", "cd")), check_vma=False
    )
```

profile of v0, /device:TPU:1, one launch (start us, length us, event | category | flops | bytes accessed | tf_op | source)
XLA Modules:
  0.0 269.0 jit_solution(3929936494071455766)
XLA Ops:
  6.5 0.0 copy-start.1
  6.5 0.0 copy-start
  6.5 0.0 all-gather.3.cloned.1.call-start
  6.5 0.7 all-gather.3.cloned.1.call-update
  7.3 0.0 reduce-scatter.2.cloned.1.call-start
  7.3 8.0 %copy.29 = bf16[4,50,800]{0,2,1:T(8,128)(2,1)} copy(bf16[4,50,800]{2,0,1:T(4,128)(2,1)} %param.6) | data formatting | bytes 640000 | tf_op args[1]
  15.9 0.0 copy-done.1
  15.9 0.0 copy-done
  16.0 10.8 %gather_fusion = bf16[2048,4]{1,0:T(8,128)(2,1)S(1)} fusion(bf16[4,40000]{0,1:T(8,128)(2,1)} %bitcast.9, s32[2048]{0:T(1024)S(1)} %get-tuple-element.7), kind=kCustom, calls=%fused_computation | custom fusion | bytes 40960 | tf_op jit(solution)/shard_map/jit(_take)/gather | solution.py:15
  26.8 0.2 copy.30
  27.0 71.2 %all-gather.3.cloned.1.call-done = bf16[4,800,800]{2,0,1:T(4,128)(2,1)} async-done(((bf16[4,50,800]{2,0,1:T(4,128)(2,1)}), bf16[4,800,800]{2,0,1:T(4,128)(2,1)}) %all-gather.3.cloned.1.call-update) | async-done | bytes 5120016 | tf_op jit(solution)/shard_map/all_gather | solution.py:16
  98.3 5.8 %copy.31 = bf16[4,800,800]{2,1,0:T(8,128)(2,1)} copy(bf16[4,800,800]{2,0,1:T(4,128)(2,1)} %all-gather.3.cloned.1.call-done) | data formatting | bytes 10240000 | tf_op jit(solution)/shard_map/all_gather | solution.py:16
  104.1 12.8 %reshape.39 = bf16[2560000]{0:T(1024)(128)(2,1)} reshape(bf16[4,800,800]{2,1,0:T(8,128)(2,1)} %copy.31) | data formatting | bytes 10240000
  116.9 6.6 %reshape.18 = bf16[4,640000]{1,0:T(4,128)(2,1)} reshape(bf16[2560000]{0:T(1024)(128)(2,1)} %reshape.39) | data formatting | bytes 10240000 | tf_op jit(solution)/shard_map/reshape | solution.py:17
  123.5 23.3 %gather_fusion.1 = bf16[2048,4]{0,1:T(4,128)(2,1)S(1)} fusion(bf16[4,640000]{1,0:T(4,128)(2,1)} %reshape.18, s32[2048]{0:T(1024)S(1)} %get-tuple-element.8), kind=kCustom, calls=%fused_computation.1 | custom fusion | bytes 40960 | tf_op jit(solution)/shard_map/jit(_take)/gather | solution.py:18
  146.8 28.2 %all-gather = bf16[16,4,2048]{2,1,0:T(4,128)(2,1)S(1)} all-gather(bf16[1,4,2048]{2,1,0:T(4,128)(2,1)S(1)} %fusion), channel_id=1, replica_groups=mesh['ab'=16,'cd'=16] {'ab'}, dimensions={0}, use_global_device_ids=true | all-gather | bytes 278528 | tf_op jit(solution)/shard_map/all_gather | solution.py:29
  175.0 0.1 reshape.38
  175.1 6.8 %fusion.1 = f32[64,2048]{1,0:T(8,128)} fusion(bf16[64,2048]{1,0:T(8,128)(2,1)S(1)} %reshape.38, bf16[2048,2048]{1,0:T(8,128)(2,1)} %param.5), kind=kOutput, calls=%fused_computation.12 | convolution fusion | flops 536870912 | bytes 9175040 | tf_op jit(solution)/shard_map/dot_general | solution.py:28
  181.9 0.0 reduce-scatter.2.cloned.1.call-update
  181.9 78.9 %reduce-scatter.2.cloned.1.call-done = f32[64,128]{1,0:T(8,128)} async-done(((f32[64,2048]{1,0:T(8,128)}), f32[64,128]{1,0:T(8,128)}) %reduce-scatter.2.cloned.1.call-update) | async-done | bytes 32784 | tf_op jit(solution)/shard_map/reduce_scatter | solution.py:34
  260.8 1.4 convert_element_type.16
  (4 shorter events, 0.1 us)
Async XLA Ops:
  6.5 9.4 %copy-start.1 = (s32[2048]{0:T(1024)S(1)}, s32[2048]{0:T(1024)}, u32[]{:S(2)}) copy-start(s32[2048]{0:T(1024)} %param.8) | copy-start | bytes 24580
  6.5 9.4 %copy-start = (s32[2048]{0:T(1024)S(1)}, s32[2048]{0:T(1024)}, u32[]{:S(2)}) copy-start(s32[2048]{0:T(1024)} %param.7) | copy-start | bytes 24580
  6.5 91.7 %all-gather.3.cloned.1.call-start = ((), (), s32[]{:S(2)}) async-start(), calls=%async_computation.1 | async-start | bytes 6092800 | tf_op jit(solution)/shard_map/all_gather | solution.py:16
  7.3 253.6 %reduce-scatter.2.cloned.1.call-start = ((), (), s32[]{:S(2)}) async-start(), calls=%async_computation.2 | async-start | bytes 557056 | tf_op jit(solution)/shard_map/reduce_scatter | solution.py:34
Sparse Core Ops, SparseCore 0:
  9.8 88.4 all-gather.2
  182.0 78.7 reduce-scatter.1
where the time goes:
time: 271 us; the launch traced here: 269 us
  waiting for transfers between devices  151 us (56%)
  local copies, waits for them, and re-layouts  67.6 us (25%)
  blocking collectives  28.2 us (10%)
  between operations  14.1 us (5%)
  matrix products  6.83 us (3%)
    reduce_scatter x1, waiting for transfers between devices, on_device(): lax.psum_scatter(partial_sums, 'cd', scatter_dimension=1, tiled=True)  78.9 us
    all_gather x1, waiting for transfers between devices, on_device(): whole = lax.all_gather(amplitudes, 'cd', axis=1, tiled=True)  71.2 us
    all_gather x1, blocking collectives, on_device(): lax.all_gather(packed, 'ab', axis=0, tiled=True)  28.2 us
    gather x1, local copies, waits for them, and re-layouts, on_device(): crossed = jnp.take(whole_flat, cd_second * orbitals + cd_first, axis=1)  23.3 us
    unnamed x7, local copies, waits for them, and re-layouts  20.9 us
    gather x2, local copies, waits for them, and re-layouts, on_device(): direct = jnp.take(own_flat, local_first * orbitals + cd_second, axis=1)  11 us
    dot_general x1, matrix products, on_device(): lax.dot_general(lax.all_gather(packed, 'ab', axis=0, tiled=True), pair_va...  6.83 us
    reshape x1, local copies, waits for them, and re-layouts, on_device(): whole_flat = whole.reshape(pair_block, orbitals * orbitals)  6.61 us
  transfers between devices with their start and end apart: 2, of which 2 were waited for; matrix products, arithmetic and copies ran while one was open for 7% of the time, Pallas kernels for 0%

commit v1 on v0

--- a/solution.py
+++ b/solution.py
@@ -11,19 +11,24 @@
     orbitals = amplitudes.shape[2]
     columns = cd_first.shape[0]
     local_first = cd_first - slab * orbit_block
-    own_flat = amplitudes.reshape(pair_block, orbit_block * orbitals)
-    direct = jnp.take(own_flat, local_first * orbitals + cd_second, axis=1)
-    whole = lax.all_gather(amplitudes, "cd", axis=1, tiled=True)
-    whole_flat = whole.reshape(pair_block, orbitals * orbitals)
-    crossed = jnp.take(whole_flat, cd_second * orbitals + cd_first, axis=1)
+    mirrored = lax.all_to_all(amplitudes, "cd", 2, 1, tiled=True)
+    pick_d = (lax.broadcasted_iota(jnp.int32, (orbitals, columns), 0) == cd_second[None, :]).astype(
+        amplitudes.dtype
+    )
+    direct_rows = lax.dot_general(
+        amplitudes, pick_d, (((2,), (0,)), ((), ())), preferred_element_type=jnp.float32
+    )
+    crossed_rows = lax.dot_general(
+        mirrored, pick_d, (((1,), (0,)), ((), ())), preferred_element_type=jnp.float32
+    )
+    pick_c = lax.broadcasted_iota(jnp.int32, (orbit_block, columns), 0) == local_first[None, :]
+    both = jnp.sum(jnp.where(pick_c[None], direct_rows + crossed_rows, 0.0), axis=1)
     live_count = live_cols[0]
     slots = jnp.arange(columns, dtype=jnp.int32)
     live = (slots < live_count).astype(jnp.float32)
     half = jnp.where(cd_first == cd_second, jnp.float32(0.5), jnp.float32(1.0))
     weight = half * live
-    packed = ((direct.astype(jnp.float32) + crossed.astype(jnp.float32)) * weight[None, :]).astype(
-        jnp.bfloat16
-    )
+    packed = (both * weight[None, :]).astype(jnp.bfloat16)
     contract = (((1,), (1,)), ((), ()))
     partial_sums = lax.dot_general(
         lax.all_gather(packed, "ab", axis=0, tiled=True),

time: 271 us -> 156 us (0.58)
  waiting for transfers between devices: 151 us -> 87.7 us
  local copies, waits for them, and re-layouts: 67.6 us -> 6.28 us
  starting transfers between devices: 0.04 us -> 11.6 us
  blocking collectives: 28.2 us -> 23.7 us
  matrix products: 6.83 us -> 10.1 us
    all_gather x1 -> x0, waiting for transfers between devices: 71.2 us -> none  [on_device(): whole = lax.all_gather(amplitudes, 'cd', axis=1, tiled=True)]
    gather x3 -> x0, local copies, waits for them, and re-layouts: 34.3 us -> none  [the longest x1 23.3 us: on_device(): crossed = jnp.take(whole_flat, cd_second * orbitals + cd_first, axis=1)]
    unnamed x7 -> x10, local copies, waits for them, and re-layouts: 20.9 us -> 4.89 us
    all_to_all x0 -> x1, starting transfers between devices: none -> 11.6 us  [on_device(): mirrored = lax.all_to_all(amplitudes, 'cd', 2, 1, tiled=True)]
    all_to_all x0 -> x1, waiting for transfers between devices: none -> 10.3 us  [on_device(): mirrored = lax.all_to_all(amplitudes, 'cd', 2, 1, tiled=True)]
    reshape x1 -> x0, local copies, waits for them, and re-layouts: 6.61 us -> none  [on_device(): whole_flat = whole.reshape(pair_block, orbitals * orbitals)]
    all_gather x1 -> x0, local copies, waits for them, and re-layouts: 5.82 us -> none  [on_device(): whole = lax.all_gather(amplitudes, 'cd', axis=1, tiled=True)]
    all_gather x1, blocking collectives: 28.2 us -> 23.7 us  [on_device(): lax.all_gather(packed, 'ab', axis=0, tiled=True)]
  transfers between devices with their start and end apart: 2 -> 2, of which waited for: 2 -> 2; matrix products, arithmetic and copies ran while one was open for 7% -> 0% of each run, Pallas kernels for 0% -> 0%
where the time goes in v1:
time: 156 us; the launch traced here: 155 us
  waiting for transfers between devices  87.7 us (56%)
  blocking collectives  23.7 us (15%)
  between operations  14.2 us (9%)
  starting transfers between devices  11.6 us (7%)
  matrix products  10.1 us (6%)
  local copies, waits for them, and re-layouts  6.28 us (4%)
    reduce_scatter x1, waiting for transfers between devices, on_device(): lax.psum_scatter(partial_sums, 'cd', scatter_dimension=1, tiled=True)  77.5 us
    all_gather x1, blocking collectives, on_device(): lax.all_gather(packed, 'ab', axis=0, tiled=True)  23.7 us
    all_to_all x1, starting transfers between devices, on_device(): mirrored = lax.all_to_all(amplitudes, 'cd', 2, 1, tiled=True)  11.6 us
    all_to_all x1, waiting for transfers between devices, on_device(): mirrored = lax.all_to_all(amplitudes, 'cd', 2, 1, tiled=True)  10.3 us
    dot_general x1, matrix products, on_device(): lax.dot_general(lax.all_gather(packed, 'ab', axis=0, tiled=True), pair_va...  6.83 us
    unnamed x10, local copies, waits for them, and re-layouts  4.89 us
  transfers between devices with their start and end apart: 2, of which 2 were waited for; matrix products, arithmetic and copies ran while one was open for 0% of the time, Pallas kernels for 0%

profile of v1, /device:TPU:1, one launch (start us, length us, event | category | flops | bytes accessed | tf_op | source)
XLA Modules:
  0.0 155.0 jit_solution(14329860062865559062)
XLA Ops:
  6.5 0.0 copy-start.2
  6.5 0.0 copy-start.1
  6.5 2.1 %copy.16 = bf16[4,50,800]{1,0,2:T(4,128)(2,1)S(1)} copy(bf16[4,50,800]{2,0,1:T(4,128)(2,1)} %param.6) | data formatting | bytes 640000 | tf_op args[1]
  8.7 1.8 %reshape.24 = bf16[16,2,5000]{2,1,0:T(2,128)(2,1)} reshape(bf16[800,4,50]{2,1,0:T(4,128)(2,1)S(1)} %bitcast.36) | data formatting | bytes 640000
  10.5 11.6 %all-to-all-start = ((bf16[16,2,5000]{2,1,0:T(2,128)(2,1)}), bf16[16,2,5000]{2,1,0:T(2,128)(2,1)S(1)}, u32[]{:S(2)}, u32[]{:S(2)}) async-start(bf16[16,2,5000]{2,1,0:T(2,128)(2,1)} %reshape.24), calls=%async_computation | async-start | bytes 655360 | tf_op jit(solution)/shard_map/all_to_all | solution.py:14
  22.1 0.0 reduce-scatter.2.cloned.1.call-start
  22.8 0.0 copy-done.2
  22.8 0.0 copy-done.1
  22.8 0.1 iota_compare_fusion.1
  22.9 10.3 %all-to-all-done = bf16[16,2,5000]{2,1,0:T(2,128)(2,1)S(1)} async-done(((bf16[16,2,5000]{2,1,0:T(2,128)(2,1)}), bf16[16,2,5000]{2,1,0:T(2,128)(2,1)S(1)}, u32[]{:S(2)}, u32[]{:S(2)}) %all-to-all-start) | async-done | bytes 320032 | tf_op jit(solution)/shard_map/all_to_all | solution.py:14
  33.2 0.9 reshape.25
  34.0 0.2 copy.24
  34.2 1.2 all_to_all.16
  35.4 0.0 copy-start
  35.4 1.6 %fusion.1 = f32[2048,4,50]{0,2,1:T(8,128)S(1)} fusion(s32[2048]{0:T(1024)S(1)} %copy-done.2, bf16[4,800,50]{1,0,2:T(4,128)(2,1)S(1)} %all_to_all.16), kind=kOutput, calls=%fused_computation.2 | convolution fusion | flops 656998400 | bytes 1966592 | tf_op jit(solution)/shard_map/dot_general | solution.py:21
  37.0 0.0 copy-done
  37.1 1.7 %fusion.16 = f32[4,2048]{1,0:T(4,128)S(1)} fusion(f32[2048,4,50]{0,2,1:T(8,128)S(1)} %fusion.1, s32[2048]{0:T(1024)S(1)} %copy-done.2, pred[50,2048]{1,0:T(8,128)(4,1)S(1)} %iota_compare_fusion.1, bf16[4,50,800]{2,0,1:T(4,128)(2,1)S(1)} %copy-done), kind=kOutput, calls=%fused_computation.9 | convolution fusion | flops 658219008 | bytes 2101760 | tf_op jit(solution)/shard_map/dot_general | solution.py:18
  38.8 23.7 %all-gather = bf16[16,4,2048]{2,1,0:T(4,128)(2,1)S(1)} all-gather(bf16[1,4,2048]{2,1,0:T(4,128)(2,1)S(1)} %fusion.21), channel_id=1, replica_groups=mesh['ab'=16,'cd'=16] {'ab'}, dimensions={0}, use_global_device_ids=true | all-gather | bytes 278528 | tf_op jit(solution)/shard_map/all_gather | solution.py:34
  62.5 0.1 reshape.22
  62.5 6.8 %fusion.22 = f32[64,2048]{1,0:T(8,128)} fusion(bf16[64,2048]{1,0:T(8,128)(2,1)S(1)} %reshape.22, bf16[2048,2048]{1,0:T(8,128)(2,1)} %param.5), kind=kOutput, calls=%fused_computation.19 | convolution fusion | flops 536870912 | bytes 9175040 | tf_op jit(solution)/shard_map/dot_general | solution.py:33
  69.4 0.0 reduce-scatter.2.cloned.1.call-update
  69.4 77.5 %reduce-scatter.2.cloned.1.call-done = f32[64,128]{1,0:T(8,128)} async-done(((f32[64,2048]{1,0:T(8,128)}), f32[64,128]{1,0:T(8,128)}) %reduce-scatter.2.cloned.1.call-update) | async-done | bytes 32784 | tf_op jit(solution)/shard_map/reduce_scatter | solution.py:39
  146.8 1.4 convert_element_type.9
  (3 shorter events, 0.0 us)
Async XLA Ops:
  6.5 16.3 %copy-start.2 = (s32[2048]{0:T(1024)S(1)}, s32[2048]{0:T(1024)}, u32[]{:S(2)}) copy-start(s32[2048]{0:T(1024)} %param.8) | copy-start | bytes 24580
  6.5 16.3 %copy-start.1 = (s32[2048]{0:T(1024)S(1)}, s32[2048]{0:T(1024)}, u32[]{:S(2)}) copy-start(s32[2048]{0:T(1024)} %param.7) | copy-start | bytes 24580
  10.5 22.7 %all-to-all-start = ((bf16[16,2,5000]{2,1,0:T(2,128)(2,1)}), bf16[16,2,5000]{2,1,0:T(2,128)(2,1)S(1)}, u32[]{:S(2)}, u32[]{:S(2)}) async-start(bf16[16,2,5000]{2,1,0:T(2,128)(2,1)} %reshape.24), calls=%async_computation | async-start | bytes 655360 | tf_op jit(solution)/shard_map/all_to_all | solution.py:14
  22.1 124.7 %reduce-scatter.2.cloned.1.call-start = ((), (), s32[]{:S(2)}) async-start(), calls=%async_computation.2 | async-start | bytes 557056 | tf_op jit(solution)/shard_map/reduce_scatter | solution.py:39
  35.4 1.6 %copy-start = (bf16[4,50,800]{2,0,1:T(4,128)(2,1)S(1)}, bf16[4,50,800]{2,0,1:T(4,128)(2,1)}, u32[]{:S(2)}) copy-start(bf16[4,50,800]{2,0,1:T(4,128)(2,1)} %param.6) | copy-start | bytes 960004
Sparse Core Ops, SparseCore 0:
  69.5 77.2 reduce-scatter.1

commit v2 on v1

--- a/solution.py
+++ b/solution.py
@@ -1,12 +1,152 @@
+import functools
+
 import jax
 import jax.numpy as jnp
 from jax import lax
+from jax.experimental import pallas as pl
+from jax.experimental.pallas import tpu as pltpu
 from jax.sharding import PartitionSpec as P
 
+MESH = pl.DeviceIdType.MESH
 
-def on_device(pair_values, amplitudes, cd_first, cd_second, live_cols):
+
+def ladder_kernel(
+    n_ab, n_cd, packed_ref, values_hbm, out_ref,
+    slots, gathered, values_buf, sums_out, sums_in,
+    values_sem, pk_send, pk_recv, sum_send, sum_recv, own_sem,
+):
+    me_ab = lax.axis_index("ab")
+    me_cd = lax.axis_index("cd")
+    rows = packed_ref.shape[0]
+    block = values_buf.shape[1]
+
+    for step in range(n_cd):
+        dest = lax.rem(me_cd + 1 + step, n_cd)
+        pltpu.make_async_copy(
+            values_hbm.at[pl.ds(pl.multiple_of(dest * block, block), block), :],
+            values_buf.at[step],
+            values_sem.at[step],
+        ).start()
+
+    barrier = pltpu.get_barrier_semaphore()
+    for k in range(1, n_ab):
+        peer = lax.rem(me_ab + k, n_ab)
+        pl.semaphore_signal(barrier, inc=1, device_id=(peer, me_cd), device_id_type=MESH)
+    for k in range(1, n_cd):
+        peer = lax.rem(me_cd + k, n_cd)
+        pl.semaphore_signal(barrier, inc=1, device_id=(me_ab, peer), device_id_type=MESH)
+    pl.semaphore_wait(barrier, (n_ab - 1) + (n_cd - 1))
+
+    own = pltpu.make_async_copy(packed_ref, slots.at[me_ab], own_sem.at[0])
+    own.start()
+    for k in range(1, n_ab):
+        peer = lax.rem(me_ab + k, n_ab)
+        pltpu.make_async_remote_copy(
+            src_ref=packed_ref,
+            dst_ref=slots.at[me_ab],
+            send_sem=pk_send.at[k],
+            recv_sem=pk_recv.at[me_ab],
+            device_id=(peer, me_cd),
+            device_id_type=MESH,
+        ).start()
+    own.wait()
+    for k in range(1, n_ab):
+        src = lax.rem(me_ab + n_ab - k, n_ab)
+        pltpu.make_async_remote_copy(
+            src_ref=packed_ref,
+            dst_ref=slots.at[src],
+            send_sem=pk_send.at[k],
+            recv_sem=pk_recv.at[src],
+            device_id=(src, me_cd),
+            device_id_type=MESH,
+        ).wait_recv()
+    for k in range(n_ab):
+        gathered[k * rows:(k + 1) * rows, :] = slots[k].astype(jnp.float32)
+    lhs = gathered[...].astype(jnp.bfloat16)
+
+    def one_block(step):
+        pltpu.make_async_copy(
+            values_hbm.at[pl.ds(0, block), :], values_buf.at[step], values_sem.at[step]
+        ).wait()
+        return lax.dot_general(
+            lhs, values_buf[step], (((1,), (1,)), ((), ())), preferred_element_type=jnp.float32
+        )
+
+    for step in range(n_cd - 1):
+        dest = lax.rem(me_cd + 1 + step, n_cd)
+        sums_out[step] = one_block(step)
+        pltpu.make_async_remote_copy(
+            src_ref=sums_out.at[step],
+            dst_ref=sums_in.at[me_cd],
+            send_sem=sum_send.at[step],
+            recv_sem=sum_recv.at[me_cd],
+            device_id=(me_ab, dest),
+            device_id_type=MESH,
+        ).start()
+    total = one_block(n_cd - 1)
+    for step in range(n_cd - 1):
+        src = lax.rem(me_cd + n_cd - 1 - step, n_cd)
+        pltpu.make_async_remote_copy(
+            src_ref=sums_out.at[step],
+            dst_ref=sums_in.at[src],
+            send_sem=sum_send.at[step],
+            recv_sem=sum_recv.at[src],
+            device_id=(me_ab, src),
+            device_id_type=MESH,
+        ).wait_recv()
+        total = total + sums_in[src]
+    out_ref[...] = total.astype(out_ref.dtype)
+
+    for k in range(1, n_ab):
+        pltpu.make_async_remote_copy(
+            src_ref=packed_ref,
+            dst_ref=slots.at[me_ab],
+            send_sem=pk_send.at[k],
+            recv_sem=pk_recv.at[me_ab],
+            device_id=(me_ab, me_cd),
+            device_id_type=MESH,
+        ).wait_send()
+    for step in range(n_cd - 1):
+        pltpu.make_async_remote_copy(
+            src_ref=sums_out.at[step],
+            dst_ref=sums_in.at[me_cd],
+            send_sem=sum_send.at[step],
+            recv_sem=sum_recv.at[me_cd],
+            device_id=(me_ab, me_cd),
+            device_id_type=MESH,
+        ).wait_send()
+
+
+def ladder(packed, pair_values, n_ab, n_cd):
+    rows, columns = packed.shape
+    ab_dev = pair_values.shape[0]
+    block = ab_dev // n_cd
+    return pl.pallas_call(
+        functools.partial(ladder_kernel, n_ab, n_cd),
+        out_shape=jax.ShapeDtypeStruct((rows * n_ab, block), jnp.bfloat16),
+        in_specs=[pl.BlockSpec(memory_space=pltpu.VMEM), pl.BlockSpec(memory_space=pl.ANY)],
+        out_specs=pl.BlockSpec(memory_space=pltpu.VMEM),
+        scratch_shapes=[
+            pltpu.VMEM((n_ab, rows, columns), packed.dtype),
+            pltpu.VMEM((rows * n_ab, columns), jnp.float32),
+            pltpu.VMEM((n_cd, block, columns), pair_values.dtype),
+            pltpu.VMEM((n_cd - 1, rows * n_ab, block), jnp.float32),
+            pltpu.VMEM((n_cd, rows * n_ab, block), jnp.float32),
+            pltpu.SemaphoreType.DMA((n_cd,)),
+            pltpu.SemaphoreType.DMA((n_ab,)),
+            pltpu.SemaphoreType.DMA((n_ab,)),
+            pltpu.SemaphoreType.DMA((n_cd,)),
+            pltpu.SemaphoreType.DMA((n_cd,)),
+            pltpu.SemaphoreType.DMA((1,)),
+        ],
+        compiler_params=pltpu.CompilerParams(
+            collective_id=0, has_side_effects=True, vmem_limit_bytes=48 * 1024 * 1024
+        ),
+    )(packed, pair_values)
+
+
+def on_device(n_ab, n_cd, pair_values, amplitudes, cd_first, cd_second, live_cols):
     slab = lax.axis_index("cd")
-    pair_block = amplitudes.shape[0]
     orbit_block = amplitudes.shape[1]
     orbitals = amplitudes.shape[2]
     columns = cd_first.shape[0]
@@ -29,20 +169,12 @@
     half = jnp.where(cd_first == cd_second, jnp.float32(0.5), jnp.float32(1.0))
     weight = half * live
     packed = (both * weight[None, :]).astype(jnp.bfloat16)
-    contract = (((1,), (1,)), ((), ()))
-    partial_sums = lax.dot_general(
-        lax.all_gather(packed, "ab", axis=0, tiled=True),
-        pair_values,
-        contract,
-        preferred_element_type=jnp.float32,
-    )
-    return lax.psum_scatter(partial_sums, "cd", scatter_dimension=1, tiled=True).astype(
-        jnp.bfloat16
-    )
+    return ladder(packed, pair_values, n_ab, n_cd)
 
 
 def solution(mesh):
     placed = (P("ab", "cd"), P("ab", "cd", None), P("cd"), P("cd"), P("cd"))
     return jax.shard_map(
-        on_device, mesh=mesh, in_specs=placed, out_specs=P(None, ("ab", "cd")), check_vma=False
+        functools.partial(on_device, mesh.shape["ab"], mesh.shape["cd"]),
+        mesh=mesh, in_specs=placed, out_specs=P(None, ("ab", "cd")), check_vma=False,
     )

time: 156 us -> 63.3 us (0.41)
  waiting for transfers between devices: 87.7 us -> 10.3 us
  Pallas kernels: 0 us -> 29.7 us
  blocking collectives: 23.7 us -> 0 us
  between operations: 14.2 us -> 0.77 us
  matrix products: 10.1 us -> 3.29 us
    reduce_scatter x1 -> x0, waiting for transfers between devices: 77.5 us -> none  [on_device(): lax.psum_scatter(partial_sums, 'cd', scatter_dimension=1, tiled=True)]
    pallas_call x0 -> x1, Pallas kernels: none -> 29.7 us  [ladder(): pl.pallas_call(functools.partial(ladder_kernel, n_ab, n_cd), out_shape=ja...]
    all_gather x1 -> x0, blocking collectives: 23.7 us -> none  [on_device(): lax.all_gather(packed, 'ab', axis=0, tiled=True)]
    dot_general x1 -> x0, matrix products: 6.83 us -> none  [on_device(): lax.dot_general(lax.all_gather(packed, 'ab', axis=0, tiled=True), pair_va...]
  transfers between devices with their start and end apart: 2 -> 1, of which waited for: 2 -> 1; matrix products, arithmetic and copies ran while one was open for 0% -> 0% of each run, Pallas kernels for 0% -> 0%
where the time goes in v2:
time: 63.3 us; the launch traced here: 62.6 us
  Pallas kernels  29.7 us (47%)
  starting transfers between devices  11.6 us (18%)
  waiting for transfers between devices  10.3 us (16%)
  local copies, waits for them, and re-layouts  6.83 us (11%)
  matrix products  3.29 us (5%)
  between operations  0.77 us (1%)
    pallas_call x1, Pallas kernels, ladder(): pl.pallas_call(functools.partial(ladder_kernel, n_ab, n_cd), out_shape=ja...  29.7 us
    all_to_all x1, starting transfers between devices, on_device(): mirrored = lax.all_to_all(amplitudes, 'cd', 2, 1, tiled=True)  11.6 us
    all_to_all x1, waiting for transfers between devices, on_device(): mirrored = lax.all_to_all(amplitudes, 'cd', 2, 1, tiled=True)  10.3 us
    unnamed x10, local copies, waits for them, and re-layouts  5.44 us
    dot_general x1, matrix products, on_device(): lax.dot_general(amplitudes, pick_d, (((2,), (0,)), ((), ())), preferred_e...  1.69 us
    dot_general x1, matrix products, on_device(): lax.dot_general(mirrored, pick_d, (((1,), (0,)), ((), ())), preferred_ele...  1.6 us
    all_to_all x2, local copies, waits for them, and re-layouts, on_device(): mirrored = lax.all_to_all(amplitudes, 'cd', 2, 1, tiled=True)  1.39 us
  transfers between devices with their start and end apart: 1, of which 1 were waited for; matrix products, arithmetic and copies ran while one was open for 0% of the time, Pallas kernels for 0%

profile of v2, /device:TPU:1, one launch (start us, length us, event | category | flops | bytes accessed | tf_op | source)
XLA Modules:
  0.0 62.6 jit_solution(11516188330443467015)
XLA Ops:
  0.0 0.0 copy-start.2
  0.0 0.0 copy-start.1
  0.0 2.1 %copy.16 = bf16[4,50,800]{1,0,2:T(4,128)(2,1)S(1)} copy(bf16[4,50,800]{2,0,1:T(4,128)(2,1)} %param.6) | data formatting | bytes 640000 | tf_op args[1]
  2.2 1.8 %reshape.22 = bf16[16,2,5000]{2,1,0:T(2,128)(2,1)} reshape(bf16[800,4,50]{2,1,0:T(4,128)(2,1)S(1)} %bitcast.32) | data formatting | bytes 640000
  4.0 11.6 %all-to-all-start = ((bf16[16,2,5000]{2,1,0:T(2,128)(2,1)}), bf16[16,2,5000]{2,1,0:T(2,128)(2,1)S(1)}, u32[]{:S(2)}, u32[]{:S(2)}) async-start(bf16[16,2,5000]{2,1,0:T(2,128)(2,1)} %reshape.22), calls=%async_computation | async-start | bytes 655360 | tf_op jit(solution)/shard_map/all_to_all | solution.py:154
  16.2 0.0 copy-done.2
  16.2 0.0 copy-done.1
  16.3 0.1 iota_compare_fusion.1
  16.3 10.3 %all-to-all-done = bf16[16,2,5000]{2,1,0:T(2,128)(2,1)S(1)} async-done(((bf16[16,2,5000]{2,1,0:T(2,128)(2,1)}), bf16[16,2,5000]{2,1,0:T(2,128)(2,1)S(1)}, u32[]{:S(2)}, u32[]{:S(2)}) %all-to-all-start) | async-done | bytes 320032 | tf_op jit(solution)/shard_map/all_to_all | solution.py:154
  26.6 0.9 %reshape.23 = bf16[800,4,50]{2,1,0:T(4,128)(2,1)S(1)} reshape(bf16[16,2,5000]{2,1,0:T(2,128)(2,1)S(1)} %all-to-all-done) | data formatting | bytes 640000
  27.5 0.2 copy.24
  27.7 1.2 %all_to_all.16 = bf16[4,800,50]{1,0,2:T(4,128)(2,1)S(1)} reshape(bf16[4,16,50,50]{2,1,0,3:T(8,128)(2,1)S(1)} %bitcast.31) | data formatting | bytes 640000 | tf_op jit(solution)/shard_map/all_to_all | solution.py:154
  28.9 0.0 copy-start
  28.9 1.6 %fusion.1 = f32[2048,4,50]{0,2,1:T(8,128)S(1)} fusion(s32[2048]{0:T(1024)S(1)} %copy-done.2, bf16[4,800,50]{1,0,2:T(4,128)(2,1)S(1)} %all_to_all.16), kind=kOutput, calls=%fused_computation.2 | convolution fusion | flops 656998400 | bytes 1966592 | tf_op jit(solution)/shard_map/dot_general | solution.py:161
  30.5 0.0 copy-done
  30.5 1.7 %fusion.16 = f32[4,2048]{1,0:T(4,128)S(1)} fusion(f32[2048,4,50]{0,2,1:T(8,128)S(1)} %fusion.1, s32[2048]{0:T(1024)S(1)} %copy-done.2, pred[50,2048]{1,0:T(8,128)(4,1)S(1)} %iota_compare_fusion.1, bf16[4,50,800]{2,0,1:T(4,128)(2,1)S(1)} %copy-done), kind=kOutput, calls=%fused_computation.9 | convolution fusion | flops 658219008 | bytes 2101760 | tf_op jit(solution)/shard_map/dot_general | solution.py:158
  32.2 29.7 %shard_map.55 = bf16[64,128]{1,0:T(8,128)(2,1)S(1)} custom-call(bf16[4,2048]{1,0:T(4,128)(2,1)S(1)} %multiply_convert_fusion.packed_ref, bf16[2048,2048]{1,0:T(8,128)(2,1)} %values_hbm.1), custom_call_target="tpu_custom_call" | custom-call | tf_op jit(solution)/shard_map/pallas_call | solution.py:124
  61.9 0.6 copy.27
  (3 shorter events, 0.0 us)
Async XLA Ops:
  0.0 16.2 %copy-start.2 = (s32[2048]{0:T(1024)S(1)}, s32[2048]{0:T(1024)}, u32[]{:S(2)}) copy-start(s32[2048]{0:T(1024)} %param.8) | copy-start | bytes 24580
  0.0 16.2 %copy-start.1 = (s32[2048]{0:T(1024)S(1)}, s32[2048]{0:T(1024)}, u32[]{:S(2)}) copy-start(s32[2048]{0:T(1024)} %param.7) | copy-start | bytes 24580
  4.0 22.7 %all-to-all-start = ((bf16[16,2,5000]{2,1,0:T(2,128)(2,1)}), bf16[16,2,5000]{2,1,0:T(2,128)(2,1)S(1)}, u32[]{:S(2)}, u32[]{:S(2)}) async-start(bf16[16,2,5000]{2,1,0:T(2,128)(2,1)} %reshape.22), calls=%async_computation | async-start | bytes 655360 | tf_op jit(solution)/shard_map/all_to_all | solution.py:154
  28.9 1.6 %copy-start = (bf16[4,50,800]{2,0,1:T(4,128)(2,1)S(1)}, bf16[4,50,800]{2,0,1:T(4,128)(2,1)}, u32[]{:S(2)}) copy-start(bf16[4,50,800]{2,0,1:T(4,128)(2,1)} %param.6) | copy-start | bytes 960004

commit v3 on v2

--- a/solution.py
+++ b/solution.py
@@ -8,6 +8,65 @@
 from jax.sharding import PartitionSpec as P
 
 MESH = pl.DeviceIdType.MESH
+
+
+def exchange_kernel(n_cd, chunks_ref, out_ref, landed, send_sem, recv_sem, own_sem):
+    me_ab = lax.axis_index("ab")
+    me_cd = lax.axis_index("cd")
+    barrier = pltpu.get_barrier_semaphore()
+    for k in range(1, n_cd):
+        peer = lax.rem(me_cd + k, n_cd)
+        pl.semaphore_signal(barrier, inc=1, device_id=(me_ab, peer), device_id_type=MESH)
+    pl.semaphore_wait(barrier, n_cd - 1)
+    own = pltpu.make_async_copy(chunks_ref.at[me_cd], landed.at[me_cd], own_sem.at[0])
+    own.start()
+    for k in range(1, n_cd):
+        peer = lax.rem(me_cd + k, n_cd)
+        pltpu.make_async_remote_copy(
+            src_ref=chunks_ref.at[peer],
+            dst_ref=landed.at[me_cd],
+            send_sem=send_sem.at[k],
+            recv_sem=recv_sem.at[me_cd],
+            device_id=(me_ab, peer),
+            device_id_type=MESH,
+        ).start()
+    own.wait()
+    for k in range(1, n_cd):
+        src = lax.rem(me_cd + n_cd - k, n_cd)
+        pltpu.make_async_remote_copy(
+            src_ref=chunks_ref.at[src],
+            dst_ref=landed.at[src],
+            send_sem=send_sem.at[k],
+            recv_sem=recv_sem.at[src],
+            device_id=(me_ab, src),
+            device_id_type=MESH,
+        ).wait_recv()
+    out_ref[...] = landed[...]
+    for k in range(1, n_cd):
+        pltpu.make_async_remote_copy(
+            src_ref=chunks_ref.at[me_cd],
+            dst_ref=landed.at[me_cd],
+            send_sem=send_sem.at[k],
+            recv_sem=recv_sem.at[me_cd],
+            device_id=(me_ab, me_cd),
+            device_id_type=MESH,
+        ).wait_send()
+
+
+def exchange(chunks, n_cd):
+    return pl.pallas_call(
+        functools.partial(exchange_kernel, n_cd),
+        out_shape=jax.ShapeDtypeStruct(chunks.shape, chunks.dtype),
+        in_specs=[pl.BlockSpec(memory_space=pltpu.VMEM)],
+        out_specs=pl.BlockSpec(memory_space=pltpu.VMEM),
+        scratch_shapes=[
+            pltpu.VMEM(chunks.shape, chunks.dtype),
+            pltpu.SemaphoreType.DMA((n_cd,)),
+            pltpu.SemaphoreType.DMA((n_cd,)),
+            pltpu.SemaphoreType.DMA((1,)),
+        ],
+        compiler_params=pltpu.CompilerParams(collective_id=1, has_side_effects=True),
+    )(chunks)
 
 
 def ladder_kernel(
@@ -151,7 +210,13 @@
     orbitals = amplitudes.shape[2]
     columns = cd_first.shape[0]
     local_first = cd_first - slab * orbit_block
-    mirrored = lax.all_to_all(amplitudes, "cd", 2, 1, tiled=True)
+    pair_block = amplitudes.shape[0]
+    piece = pair_block * orbit_block * orbit_block
+    padded = -(-piece // 1024) * 1024
+    chunks = jnp.transpose(amplitudes.reshape(pair_block, orbit_block, n_cd, orbit_block), (2, 0, 1, 3))
+    chunks = jnp.pad(chunks.reshape(n_cd, piece), ((0, 0), (0, padded - piece)))
+    landed = exchange(chunks.reshape(n_cd, padded // 128, 128), n_cd)
+    mirrored = landed.reshape(n_cd, padded)[:, :piece].reshape(n_cd, pair_block, orbit_block, orbit_block)
     pick_d = (lax.broadcasted_iota(jnp.int32, (orbitals, columns), 0) == cd_second[None, :]).astype(
         amplitudes.dtype
     )
@@ -159,7 +224,10 @@
         amplitudes, pick_d, (((2,), (0,)), ((), ())), preferred_element_type=jnp.float32
     )
     crossed_rows = lax.dot_general(
-        mirrored, pick_d, (((1,), (0,)), ((), ())), preferred_element_type=jnp.float32
+        mirrored,
+        pick_d.reshape(n_cd, orbit_block, columns),
+        (((0, 2), (0, 1)), ((), ())),
+        preferred_element_type=jnp.float32,
     )
     pick_c = lax.broadcasted_iota(jnp.int32, (orbit_block, columns), 0) == local_first[None, :]
     both = jnp.sum(jnp.where(pick_c[None], direct_rows + crossed_rows, 0.0), axis=1)

time: 63.3 us -> 64.1 us (1.013)
  the two profiles are of different devices: /device:TPU:1 before, /device:TPU:6 now
where the time goes in v3:
time: 64.1 us; the launch traced here: 63.9 us
  Pallas kernels  52 us (81%)
  local copies, waits for them, and re-layouts  7.66 us (12%)
  matrix products  3.43 us (5%)
  between operations  0.81 us (1%)
    pallas_call x1, Pallas kernels, ladder(): pl.pallas_call(functools.partial(ladder_kernel, n_ab, n_cd), out_shape=ja...  32.7 us
    pallas_call x1, Pallas kernels, exchange(): pl.pallas_call(functools.partial(exchange_kernel, n_cd), out_shape=jax.Sh...  19.3 us
    reshape x2, local copies, waits for them, and re-layouts, on_device(): amplitudes.reshape(pair_block, orbit_block, n_cd, orbit_block)  2.99 us
    unnamed x10, local copies, waits for them, and re-layouts  2.47 us
    dot_general x1, matrix products, on_device(): lax.dot_general(mirrored, pick_d.reshape(n_cd, orbit_block, columns), (((...  1.74 us
    dot_general x1, matrix products, on_device(): lax.dot_general(amplitudes, pick_d, (((2,), (0,)), ((), ())), preferred_e...  1.69 us
    reshape x1, local copies, waits for them, and re-layouts, on_device(): landed.reshape(n_cd, padded)[:, :piece]  1.32 us

profile of v3, /device:TPU:6, one launch (start us, length us, event | category | flops | bytes accessed | tf_op | source)
XLA Modules:
  0.0 63.9 jit_solution(3737737508350083641)
XLA Ops:
  0.0 2.5 %reshape.53 = bf16[4,50,16,50]{3,2,0,1:T(8,128)(2,1)S(1)} reshape(bf16[4,50,800]{2,0,1:T(4,128)(2,1)} %param.6) | data formatting | bytes 640000 | tf_op jit(solution)/shard_map/reshape | solution.py:216
  2.5 0.5 copy.19
  3.0 0.8 %reshape.54 = bf16[16,10000]{1,0:T(8,128)(2,1)S(1)} reshape(bf16[16,4,50,50]{3,2,1,0:T(8,128)(2,1)S(1)} %bitcast.43) | data formatting | bytes 640000 | tf_op jit(solution)/shard_map/reshape | solution.py:217
  3.9 0.0 copy-start.1
  3.9 0.8 %copy.13 = bf16[2,8,80,128]{3,2,1,0:T(8,128)(2,1)} copy(bf16[2,8,80,128]{3,1,2,0:T(8,128)(2,1)S(1)} %pad_bitcast_fusion) | data formatting | bytes 655360
  4.7 19.3 %shard_map.55 = bf16[16,80,128]{2,1,0:T(8,128)(2,1)} custom-call(bf16[16,80,128]{2,1,0:T(8,128)(2,1)} %bitcast.44), custom_call_target="tpu_custom_call" | custom-call | tf_op jit(solution)/shard_map/pallas_call | solution.py:57
  23.9 1.1 %copy.20 = bf16[2,8,80,128]{3,1,2,0:T(8,128)(2,1)S(1)} copy(bf16[2,8,80,128]{3,2,1,0:T(8,128)(2,1)} %bitcast.45) | data formatting | bytes 655360
  25.0 0.0 copy-start.2
  25.0 0.0 copy-start
  25.1 1.3 %reshape.57 = bf16[16,4,50,50]{3,2,1,0:T(8,128)(2,1)S(1)} reshape(bf16[16,10000]{1,0:T(8,128)(2,1)S(1)} %slice.4) | data formatting | bytes 640000 | tf_op jit(solution)/shard_map/reshape | solution.py:219
  26.4 0.0 copy-done.1
  26.4 1.7 %fusion.9 = f32[4,50,2048]{2,1,0:T(8,128)S(1)} fusion(bf16[16,4,50,50]{3,2,1,0:T(8,128)(2,1)S(1)} %reshape.57, s32[2048]{0:T(1024)S(1)} %copy-done.1, s32[16,50]{1,0:T(8,128)S(1)} %multiply_add_fusion), kind=kOutput, calls=%fused_computation.9 | convolution fusion | flops 656998400 | bytes 1969792 | tf_op jit(solution)/shard_map/dot_general | solution.py:226
  28.2 0.0 copy-done.2
  28.2 0.1 iota_compare_fusion.1
  28.2 0.0 copy-done
  28.3 1.7 %fusion.21 = f32[4,2048]{1,0:T(4,128)S(1)} fusion(f32[4,50,2048]{2,1,0:T(8,128)S(1)} %fusion.9, s32[2048]{0:T(1024)S(1)} %copy-done.1, pred[50,2048]{1,0:T(8,128)(4,1)S(1)} %iota_compare_fusion.1, bf16[4,50,800]{2,0,1:T(4,128)(2,1)S(1)} %copy-done), kind=kOutput, calls=%fused_computation.13 | convolution fusion | flops 658219008 | bytes 2101760 | tf_op jit(solution)/shard_map/dot_general | solution.py:223
  30.6 32.7 %shard_map.56 = bf16[64,128]{1,0:T(8,128)(2,1)S(1)} custom-call(bf16[4,2048]{1,0:T(4,128)(2,1)S(1)} %multiply_convert_fusion.packed_ref, bf16[2048,2048]{1,0:T(8,128)(2,1)} %values_hbm.1), custom_call_target="tpu_custom_call" | custom-call | tf_op jit(solution)/shard_map/pallas_call | solution.py:183
  63.3 0.6 copy.23
  (6 shorter events, 0.1 us)
Async XLA Ops:
  3.9 22.5 %copy-start.1 = (s32[2048]{0:T(1024)S(1)}, s32[2048]{0:T(1024)}, u32[]{:S(2)}) copy-start(s32[2048]{0:T(1024)} %param.8) | copy-start | bytes 24580
  25.0 3.1 %copy-start.2 = (s32[2048]{0:T(1024)S(1)}, s32[2048]{0:T(1024)}, u32[]{:S(2)}) copy-start(s32[2048]{0:T(1024)} %param.7) | copy-start | bytes 24580
  25.0 3.2 %copy-start = (bf16[4,50,800]{2,0,1:T(4,128)(2,1)S(1)}, bf16[4,50,800]{2,0,1:T(4,128)(2,1)}, u32[]{:S(2)}) copy-start(bf16[4,50,800]{2,0,1:T(4,128)(2,1)} %param.6) | copy-start | bytes 960004

commit v4 on v3

--- a/solution.py
+++ b/solution.py
@@ -22,35 +22,54 @@
     own.start()
     for k in range(1, n_cd):
         peer = lax.rem(me_cd + k, n_cd)
-        pltpu.make_async_remote_copy(
-            src_ref=chunks_ref.at[peer],
-            dst_ref=landed.at[me_cd],
-            send_sem=send_sem.at[k],
-            recv_sem=recv_sem.at[me_cd],
-            device_id=(me_ab, peer),
-            device_id_type=MESH,
-        ).start()
+
+        @pl.when(peer < me_cd)
+        def _():
+            pltpu.make_async_remote_copy(
+                src_ref=chunks_ref.at[peer],
+                dst_ref=landed.at[me_cd],
+                send_sem=send_sem.at[k],
+                recv_sem=recv_sem.at[me_cd],
+                device_id=(me_ab, peer),
+                device_id_type=MESH,
+            ).start()
+
+    for k in range(1, n_cd):
+        src = lax.rem(me_cd + k, n_cd)
+
+        @pl.when(src < me_cd)
+        def _():
+            landed[src] = jnp.zeros(landed.shape[1:], landed.dtype)
+
     own.wait()
     for k in range(1, n_cd):
         src = lax.rem(me_cd + n_cd - k, n_cd)
-        pltpu.make_async_remote_copy(
-            src_ref=chunks_ref.at[src],
-            dst_ref=landed.at[src],
-            send_sem=send_sem.at[k],
-            recv_sem=recv_sem.at[src],
-            device_id=(me_ab, src),
-            device_id_type=MESH,
-        ).wait_recv()
+
+        @pl.when(src > me_cd)
+        def _():
+            pltpu.make_async_remote_copy(
+                src_ref=chunks_ref.at[src],
+                dst_ref=landed.at[src],
+                send_sem=send_sem.at[k],
+                recv_sem=recv_sem.at[src],
+                device_id=(me_ab, src),
+                device_id_type=MESH,
+            ).wait_recv()
+
     out_ref[...] = landed[...]
     for k in range(1, n_cd):
-        pltpu.make_async_remote_copy(
-            src_ref=chunks_ref.at[me_cd],
-            dst_ref=landed.at[me_cd],
-            send_sem=send_sem.at[k],
-            recv_sem=recv_sem.at[me_cd],
-            device_id=(me_ab, me_cd),
-            device_id_type=MESH,
-        ).wait_send()
+        peer = lax.rem(me_cd + k, n_cd)
+
+        @pl.when(peer < me_cd)
+        def _():
+            pltpu.make_async_remote_copy(
+                src_ref=chunks_ref.at[me_cd],
+                dst_ref=landed.at[me_cd],
+                send_sem=send_sem.at[k],
+                recv_sem=recv_sem.at[me_cd],
+                device_id=(me_ab, me_cd),
+                device_id_type=MESH,
+            ).wait_send()
 
 
 def exchange(chunks, n_cd):
@@ -133,7 +152,7 @@
 
     for step in range(n_cd - 1):
         dest = lax.rem(me_cd + 1 + step, n_cd)
-        sums_out[step] = one_block(step)
+        sums_out[step] = one_block(step).astype(sums_out.dtype)
         pltpu.make_async_remote_copy(
             src_ref=sums_out.at[step],
             dst_ref=sums_in.at[me_cd],
@@ -153,7 +172,7 @@
             device_id=(me_ab, src),
             device_id_type=MESH,
         ).wait_recv()
-        total = total + sums_in[src]
+        total = total + sums_in[src].astype(jnp.float32)
     out_ref[...] = total.astype(out_ref.dtype)
 
     for k in range(1, n_ab):
@@ -189,8 +208,8 @@
             pltpu.VMEM((n_ab, rows, columns), packed.dtype),
             pltpu.VMEM((rows * n_ab, columns), jnp.float32),
             pltpu.VMEM((n_cd, block, columns), pair_values.dtype),
-            pltpu.VMEM((n_cd - 1, rows * n_ab, block), jnp.float32),
-            pltpu.VMEM((n_cd, rows * n_ab, block), jnp.float32),
+            pltpu.VMEM((n_cd - 1, rows * n_ab, block), jnp.bfloat16),
+            pltpu.VMEM((n_cd, rows * n_ab, block), jnp.bfloat16),
             pltpu.SemaphoreType.DMA((n_cd,)),
             pltpu.SemaphoreType.DMA((n_ab,)),
             pltpu.SemaphoreType.DMA((n_ab,)),

time: 64.1 us -> 54.7 us (0.85)
  the two profiles are of different devices: /device:TPU:6 before, /device:TPU:1 now
where the time goes in v4:
time: 54.7 us; the launch traced here: 53.8 us
  Pallas kernels  41.9 us (77%)
  local copies, waits for them, and re-layouts  7.66 us (14%)
  matrix products  3.42 us (6%)
  between operations  0.81 us (1%)
    pallas_call x1, Pallas kernels, ladder(): pl.pallas_call(functools.partial(ladder_kernel, n_ab, n_cd), out_shape=ja...  26 us
    pallas_call x1, Pallas kernels, exchange(): pl.pallas_call(functools.partial(exchange_kernel, n_cd), out_shape=jax.Sh...  15.9 us
    reshape x2, local copies, waits for them, and re-layouts, on_device(): amplitudes.reshape(pair_block, orbit_block, n_cd, orbit_block)  2.99 us
    unnamed x10, local copies, waits for them, and re-layouts  2.47 us
    dot_general x1, matrix products, on_device(): lax.dot_general(mirrored, pick_d.reshape(n_cd, orbit_block, columns), (((...  1.73 us
    dot_general x1, matrix products, on_device(): lax.dot_general(amplitudes, pick_d, (((2,), (0,)), ((), ())), preferred_e...  1.69 us
    reshape x1, local copies, waits for them, and re-layouts, on_device(): landed.reshape(n_cd, padded)[:, :piece]  1.32 us

profile of v4, /device:TPU:1, one launch (start us, length us, event | category | flops | bytes accessed | tf_op | source)
XLA Modules:
  0.0 53.8 jit_solution(8335886451660370629)
XLA Ops:
  0.0 2.5 %reshape.53 = bf16[4,50,16,50]{3,2,0,1:T(8,128)(2,1)S(1)} reshape(bf16[4,50,800]{2,0,1:T(4,128)(2,1)} %param.6) | data formatting | bytes 640000 | tf_op jit(solution)/shard_map/reshape | solution.py:235
  2.5 0.5 %copy.19 = bf16[4,50,16,50]{3,1,0,2:T(8,128)(2,1)S(1)} copy(bf16[4,50,16,50]{3,2,0,1:T(8,128)(2,1)S(1)} %reshape.53) | data formatting | bytes 640000 | tf_op jit(solution)/shard_map/reshape | solution.py:235
  3.0 0.8 %reshape.54 = bf16[16,10000]{1,0:T(8,128)(2,1)S(1)} reshape(bf16[16,4,50,50]{3,2,1,0:T(8,128)(2,1)S(1)} %bitcast.43) | data formatting | bytes 640000 | tf_op jit(solution)/shard_map/reshape | solution.py:236
  3.9 0.0 copy-start.1
  3.9 0.8 %copy.13 = bf16[2,8,80,128]{3,2,1,0:T(8,128)(2,1)} copy(bf16[2,8,80,128]{3,1,2,0:T(8,128)(2,1)S(1)} %pad_bitcast_fusion) | data formatting | bytes 655360
  4.7 15.9 %shard_map.55 = bf16[16,80,128]{2,1,0:T(8,128)(2,1)} custom-call(bf16[16,80,128]{2,1,0:T(8,128)(2,1)} %bitcast.44), custom_call_target="tpu_custom_call" | custom-call | tf_op jit(solution)/shard_map/pallas_call | solution.py:76
  20.5 1.1 %copy.20 = bf16[2,8,80,128]{3,1,2,0:T(8,128)(2,1)S(1)} copy(bf16[2,8,80,128]{3,2,1,0:T(8,128)(2,1)} %bitcast.45) | data formatting | bytes 655360
  21.6 0.0 copy-start.2
  21.6 0.0 copy-start
  21.6 1.3 %reshape.57 = bf16[16,4,50,50]{3,2,1,0:T(8,128)(2,1)S(1)} reshape(bf16[16,10000]{1,0:T(8,128)(2,1)S(1)} %slice.4) | data formatting | bytes 640000 | tf_op jit(solution)/shard_map/reshape | solution.py:238
  23.0 0.0 copy-done.1
  23.0 1.7 %fusion.9 = f32[4,50,2048]{2,1,0:T(8,128)S(1)} fusion(bf16[16,4,50,50]{3,2,1,0:T(8,128)(2,1)S(1)} %reshape.57, s32[2048]{0:T(1024)S(1)} %copy-done.1, s32[16,50]{1,0:T(8,128)S(1)} %multiply_add_fusion), kind=kOutput, calls=%fused_computation.9 | convolution fusion | flops 656998400 | bytes 1969792 | tf_op jit(solution)/shard_map/dot_general | solution.py:245
  24.7 0.0 copy-done.2
  24.8 0.1 iota_compare_fusion.1
  24.8 0.0 copy-done
  24.8 1.7 %fusion.21 = f32[4,2048]{1,0:T(4,128)S(1)} fusion(f32[4,50,2048]{2,1,0:T(8,128)S(1)} %fusion.9, s32[2048]{0:T(1024)S(1)} %copy-done.1, pred[50,2048]{1,0:T(8,128)(4,1)S(1)} %iota_compare_fusion.1, bf16[4,50,800]{2,0,1:T(4,128)(2,1)S(1)} %copy-done), kind=kOutput, calls=%fused_computation.13 | convolution fusion | flops 658219008 | bytes 2101760 | tf_op jit(solution)/shard_map/dot_general | solution.py:242
  27.2 26.0 %shard_map.56 = bf16[64,128]{1,0:T(8,128)(2,1)S(1)} custom-call(bf16[4,2048]{1,0:T(4,128)(2,1)S(1)} %multiply_convert_fusion.packed_ref, bf16[2048,2048]{1,0:T(8,128)(2,1)} %values_hbm.1), custom_call_target="tpu_custom_call" | custom-call | tf_op jit(solution)/shard_map/pallas_call | solution.py:202
  53.2 0.6 %copy.23 = bf16[64,128]{1,0:T(8,128)(2,1)} copy(bf16[64,128]{1,0:T(8,128)(2,1)S(1)} %shard_map.56) | data formatting | bytes 32768
  (6 shorter events, 0.1 us)
Async XLA Ops:
  3.9 19.1 %copy-start.1 = (s32[2048]{0:T(1024)S(1)}, s32[2048]{0:T(1024)}, u32[]{:S(2)}) copy-start(s32[2048]{0:T(1024)} %param.8) | copy-start | bytes 24580
  21.6 3.1 %copy-start.2 = (s32[2048]{0:T(1024)S(1)}, s32[2048]{0:T(1024)}, u32[]{:S(2)}) copy-start(s32[2048]{0:T(1024)} %param.7) | copy-start | bytes 24580
  21.6 3.2 %copy-start = (bf16[4,50,800]{2,0,1:T(4,128)(2,1)S(1)}, bf16[4,50,800]{2,0,1:T(4,128)(2,1)}, u32[]{:S(2)}) copy-start(bf16[4,50,800]{2,0,1:T(4,128)(2,1)} %param.6) | copy-start | bytes 960004

commit v5 on v4

--- a/solution.py
+++ b/solution.py
@@ -8,6 +8,7 @@
 from jax.sharding import PartitionSpec as P
 
 MESH = pl.DeviceIdType.MESH
+X_CHIPS = 4
 
 
 def exchange_kernel(n_cd, chunks_ref, out_ref, landed, send_sem, recv_sem, own_sem):
@@ -89,19 +90,24 @@
 
 
 def ladder_kernel(
-    n_ab, n_cd, packed_ref, values_hbm, out_ref,
-    slots, gathered, values_buf, sums_out, sums_in,
-    values_sem, pk_send, pk_recv, sum_send, sum_recv, own_sem,
+    n_ab, n_x, n_z, packed_ref, values_hbm, out_ref,
+    slots, gathered, values_buf, first_out, first_in, second_out, second_in,
+    values_sem, pk_send, pk_recv, first_send, first_recv, second_send, second_recv, own_sem,
 ):
     me_ab = lax.axis_index("ab")
     me_cd = lax.axis_index("cd")
+    me_z = me_cd // n_x
+    me_x = lax.rem(me_cd, n_x)
     rows = packed_ref.shape[0]
     block = values_buf.shape[1]
 
-    for step in range(n_cd):
-        dest = lax.rem(me_cd + 1 + step, n_cd)
+    order = []
+    for k in list(range(1, n_x)) + [0]:
+        for z in range(n_z):
+            order.append(z * n_x + lax.rem(me_x + k, n_x))
+    for step, owner in enumerate(order):
         pltpu.make_async_copy(
-            values_hbm.at[pl.ds(pl.multiple_of(dest * block, block), block), :],
+            values_hbm.at[pl.ds(pl.multiple_of(owner * block, block), block), :],
             values_buf.at[step],
             values_sem.at[step],
         ).start()
@@ -110,10 +116,13 @@
     for k in range(1, n_ab):
         peer = lax.rem(me_ab + k, n_ab)
         pl.semaphore_signal(barrier, inc=1, device_id=(peer, me_cd), device_id_type=MESH)
-    for k in range(1, n_cd):
-        peer = lax.rem(me_cd + k, n_cd)
+    for k in range(1, n_x):
+        peer = me_z * n_x + lax.rem(me_x + k, n_x)
         pl.semaphore_signal(barrier, inc=1, device_id=(me_ab, peer), device_id_type=MESH)
-    pl.semaphore_wait(barrier, (n_ab - 1) + (n_cd - 1))
+    for j in range(1, n_z):
+        peer = lax.rem(me_z + j, n_z) * n_x + me_x
+        pl.semaphore_signal(barrier, inc=1, device_id=(me_ab, peer), device_id_type=MESH)
+    pl.semaphore_wait(barrier, (n_ab - 1) + (n_x - 1) + (n_z - 1))
 
     own = pltpu.make_async_copy(packed_ref, slots.at[me_ab], own_sem.at[0])
     own.start()
@@ -150,29 +159,60 @@
             lhs, values_buf[step], (((1,), (1,)), ((), ())), preferred_element_type=jnp.float32
         )
 
-    for step in range(n_cd - 1):
-        dest = lax.rem(me_cd + 1 + step, n_cd)
-        sums_out[step] = one_block(step).astype(sums_out.dtype)
-        pltpu.make_async_remote_copy(
-            src_ref=sums_out.at[step],
-            dst_ref=sums_in.at[me_cd],
-            send_sem=sum_send.at[step],
-            recv_sem=sum_recv.at[me_cd],
-            device_id=(me_ab, dest),
+    for k in range(1, n_x):
+        peer = me_z * n_x + lax.rem(me_x + k, n_x)
+        for z in range(n_z):
+            first_out[k - 1, z] = one_block((k - 1) * n_z + z)
+        pltpu.make_async_remote_copy(
+            src_ref=first_out.at[k - 1],
+            dst_ref=first_in.at[k - 1],
+            send_sem=first_send.at[k - 1],
+            recv_sem=first_recv.at[k - 1],
+            device_id=(me_ab, peer),
             device_id_type=MESH,
         ).start()
-    total = one_block(n_cd - 1)
-    for step in range(n_cd - 1):
-        src = lax.rem(me_cd + n_cd - 1 - step, n_cd)
-        pltpu.make_async_remote_copy(
-            src_ref=sums_out.at[step],
-            dst_ref=sums_in.at[src],
-            send_sem=sum_send.at[step],
-            recv_sem=sum_recv.at[src],
+    stage = [one_block((n_x - 1) * n_z + z) for z in range(n_z)]
+    for k in range(1, n_x):
+        src = me_z * n_x + lax.rem(me_x + n_x - k, n_x)
+        pltpu.make_async_remote_copy(
+            src_ref=first_out.at[k - 1],
+            dst_ref=first_in.at[k - 1],
+            send_sem=first_send.at[k - 1],
+            recv_sem=first_recv.at[k - 1],
             device_id=(me_ab, src),
             device_id_type=MESH,
         ).wait_recv()
-        total = total + sums_in[src].astype(jnp.float32)
+        stage = [stage[z] + first_in[k - 1, z] for z in range(n_z)]
+
+    for j in range(1, n_z):
+        dest_z = lax.rem(me_z + j, n_z)
+        peer = dest_z * n_x + me_x
+        picked = stage[0]
+        for z in range(1, n_z):
+            picked = jnp.where(dest_z == z, stage[z], picked)
+        second_out[j - 1] = picked
+        pltpu.make_async_remote_copy(
+            src_ref=second_out.at[j - 1],
+            dst_ref=second_in.at[j - 1],
+            send_sem=second_send.at[j - 1],
+            recv_sem=second_recv.at[j - 1],
+            device_id=(me_ab, peer),
+            device_id_type=MESH,
+        ).start()
+    total = stage[0]
+    for z in range(1, n_z):
+        total = jnp.where(me_z == z, stage[z], total)
+    for j in range(1, n_z):
+        src = lax.rem(me_z + n_z - j, n_z) * n_x + me_x
+        pltpu.make_async_remote_copy(
+            src_ref=second_out.at[j - 1],
+            dst_ref=second_in.at[j - 1],
+            send_sem=second_send.at[j - 1],
+            recv_sem=second_recv.at[j - 1],
+            device_id=(me_ab, src),
+            device_id_type=MESH,
+        ).wait_recv()
+        total = total + second_in[j - 1]
     out_ref[...] = total.astype(out_ref.dtype)
 
     for k in range(1, n_ab):
@@ -184,12 +224,21 @@
             device_id=(me_ab, me_cd),
             device_id_type=MESH,
         ).wait_send()
-    for step in range(n_cd - 1):
-        pltpu.make_async_remote_copy(
-            src_ref=sums_out.at[step],
-            dst_ref=sums_in.at[me_cd],
-            send_sem=sum_send.at[step],
-            recv_sem=sum_recv.at[me_cd],
+    for k in range(1, n_x):
+        pltpu.make_async_remote_copy(
+            src_ref=first_out.at[k - 1],
+            dst_ref=first_in.at[k - 1],
+            send_sem=first_send.at[k - 1],
+            recv_sem=first_recv.at[k - 1],
+            device_id=(me_ab, me_cd),
+            device_id_type=MESH,
+        ).wait_send()
+    for j in range(1, n_z):
+        pltpu.make_async_remote_copy(
+            src_ref=second_out.at[j - 1],
+            dst_ref=second_in.at[j - 1],
+            send_sem=second_send.at[j - 1],
+            recv_sem=second_recv.at[j - 1],
             device_id=(me_ab, me_cd),
             device_id_type=MESH,
         ).wait_send()
@@ -199,22 +248,29 @@
     rows, columns = packed.shape
     ab_dev = pair_values.shape[0]
     block = ab_dev // n_cd
+    n_x = X_CHIPS
+    n_z = n_cd // n_x
+    width = rows * n_ab
     return pl.pallas_call(
-        functools.partial(ladder_kernel, n_ab, n_cd),
-        out_shape=jax.ShapeDtypeStruct((rows * n_ab, block), jnp.bfloat16),
+        functools.partial(ladder_kernel, n_ab, n_x, n_z),
+        out_shape=jax.ShapeDtypeStruct((width, block), jnp.bfloat16),
         in_specs=[pl.BlockSpec(memory_space=pltpu.VMEM), pl.BlockSpec(memory_space=pl.ANY)],
         out_specs=pl.BlockSpec(memory_space=pltpu.VMEM),
         scratch_shapes=[
             pltpu.VMEM((n_ab, rows, columns), packed.dtype),
-            pltpu.VMEM((rows * n_ab, columns), jnp.float32),
+            pltpu.VMEM((width, columns), jnp.float32),
             pltpu.VMEM((n_cd, block, columns), pair_values.dtype),
-            pltpu.VMEM((n_cd - 1, rows * n_ab, block), jnp.bfloat16),
-            pltpu.VMEM((n_cd, rows * n_ab, block), jnp.bfloat16),
+            pltpu.VMEM((n_x - 1, n_z, width, block), jnp.float32),
+            pltpu.VMEM((n_x - 1, n_z, width, block), jnp.float32),
+            pltpu.VMEM((n_z - 1, width, block), jnp.float32),
+            pltpu.VMEM((n_z - 1, width, block), jnp.float32),
             pltpu.SemaphoreType.DMA((n_cd,)),
             pltpu.SemaphoreType.DMA((n_ab,)),
             pltpu.SemaphoreType.DMA((n_ab,)),
-            pltpu.SemaphoreType.DMA((n_cd,)),
-            pltpu.SemaphoreType.DMA((n_cd,)),
+            pltpu.SemaphoreType.DMA((n_x - 1,)),
+            pltpu.SemaphoreType.DMA((n_x - 1,)),
+            pltpu.SemaphoreType.DMA((n_z - 1,)),
+            pltpu.SemaphoreType.DMA((n_z - 1,)),
             pltpu.SemaphoreType.DMA((1,)),
         ],
         compiler_params=pltpu.CompilerParams(

time: 54.7 us -> 59.7 us (1.091)
  the two profiles are of different devices: /device:TPU:1 before, /device:TPU:2 now
where the time goes in v5:
time: 59.7 us; the launch traced here: 59.5 us
  Pallas kernels  47.5 us (80%)
  local copies, waits for them, and re-layouts  7.66 us (13%)
  matrix products  3.43 us (6%)
  between operations  0.81 us (1%)
    pallas_call x1, Pallas kernels, ladder(): pl.pallas_call(functools.partial(ladder_kernel, n_ab, n_x, n_z), out_shap...  29.4 us
    pallas_call x1, Pallas kernels, exchange(): pl.pallas_call(functools.partial(exchange_kernel, n_cd), out_shape=jax.Sh...  18.1 us
    reshape x2, local copies, waits for them, and re-layouts, on_device(): amplitudes.reshape(pair_block, orbit_block, n_cd, orbit_block)  2.99 us
    unnamed x10, local copies, waits for them, and re-layouts  2.47 us
    dot_general x1, matrix products, on_device(): lax.dot_general(mirrored, pick_d.reshape(n_cd, orbit_block, columns), (((...  1.74 us
    dot_general x1, matrix products, on_device(): lax.dot_general(amplitudes, pick_d, (((2,), (0,)), ((), ())), preferred_e...  1.69 us
    reshape x1, local copies, waits for them, and re-layouts, on_device(): landed.reshape(n_cd, padded)[:, :piece]  1.32 us

profile of v5, /device:TPU:2, one launch (start us, length us, event | category | flops | bytes accessed | tf_op | source)
XLA Modules:
  0.0 59.5 jit_solution(1091692209016664424)
XLA Ops:
  0.0 2.5 %reshape.53 = bf16[4,50,16,50]{3,2,0,1:T(8,128)(2,1)S(1)} reshape(bf16[4,50,800]{2,0,1:T(4,128)(2,1)} %param.6) | data formatting | bytes 640000 | tf_op jit(solution)/shard_map/reshape | solution.py:291
  2.5 0.5 copy.19
  3.0 0.8 %reshape.54 = bf16[16,10000]{1,0:T(8,128)(2,1)S(1)} reshape(bf16[16,4,50,50]{3,2,1,0:T(8,128)(2,1)S(1)} %bitcast.43) | data formatting | bytes 640000 | tf_op jit(solution)/shard_map/reshape | solution.py:292
  3.9 0.0 copy-start.1
  3.9 0.8 %copy.13 = bf16[2,8,80,128]{3,2,1,0:T(8,128)(2,1)} copy(bf16[2,8,80,128]{3,1,2,0:T(8,128)(2,1)S(1)} %pad_bitcast_fusion) | data formatting | bytes 655360
  4.7 18.1 %shard_map.55 = bf16[16,80,128]{2,1,0:T(8,128)(2,1)} custom-call(bf16[16,80,128]{2,1,0:T(8,128)(2,1)} %bitcast.44), custom_call_target="tpu_custom_call" | custom-call | tf_op jit(solution)/shard_map/pallas_call | solution.py:77
  22.8 1.1 %copy.20 = bf16[2,8,80,128]{3,1,2,0:T(8,128)(2,1)S(1)} copy(bf16[2,8,80,128]{3,2,1,0:T(8,128)(2,1)} %bitcast.45) | data formatting | bytes 655360
  23.9 0.0 copy-start.2
  23.9 0.0 copy-start
  23.9 1.3 %reshape.57 = bf16[16,4,50,50]{3,2,1,0:T(8,128)(2,1)S(1)} reshape(bf16[16,10000]{1,0:T(8,128)(2,1)S(1)} %slice.4) | data formatting | bytes 640000 | tf_op jit(solution)/shard_map/reshape | solution.py:294
  25.3 0.0 copy-done.1
  25.3 1.7 %fusion.9 = f32[4,50,2048]{2,1,0:T(8,128)S(1)} fusion(bf16[16,4,50,50]{3,2,1,0:T(8,128)(2,1)S(1)} %reshape.57, s32[2048]{0:T(1024)S(1)} %copy-done.1, s32[16,50]{1,0:T(8,128)S(1)} %multiply_add_fusion), kind=kOutput, calls=%fused_computation.9 | convolution fusion | flops 656998400 | bytes 1969792 | tf_op jit(solution)/shard_map/dot_general | solution.py:301
  27.0 0.0 copy-done.2
  27.0 0.1 iota_compare_fusion.1
  27.1 0.0 copy-done
  27.1 1.7 %fusion.21 = f32[4,2048]{1,0:T(4,128)S(1)} fusion(f32[4,50,2048]{2,1,0:T(8,128)S(1)} %fusion.9, s32[2048]{0:T(1024)S(1)} %copy-done.1, pred[50,2048]{1,0:T(8,128)(4,1)S(1)} %iota_compare_fusion.1, bf16[4,50,800]{2,0,1:T(4,128)(2,1)S(1)} %copy-done), kind=kOutput, calls=%fused_computation.13 | convolution fusion | flops 658219008 | bytes 2101760 | tf_op jit(solution)/shard_map/dot_general | solution.py:298
  29.5 29.4 %shard_map.56 = bf16[64,128]{1,0:T(8,128)(2,1)S(1)} custom-call(bf16[4,2048]{1,0:T(4,128)(2,1)S(1)} %multiply_convert_fusion.packed_ref, bf16[2048,2048]{1,0:T(8,128)(2,1)} %values_hbm.1), custom_call_target="tpu_custom_call" | custom-call | tf_op jit(solution)/shard_map/pallas_call | solution.py:254
  58.9 0.6 %copy.23 = bf16[64,128]{1,0:T(8,128)(2,1)} copy(bf16[64,128]{1,0:T(8,128)(2,1)S(1)} %shard_map.56) | data formatting | bytes 32768
  (6 shorter events, 0.1 us)
Async XLA Ops:
  3.9 21.4 %copy-start.1 = (s32[2048]{0:T(1024)S(1)}, s32[2048]{0:T(1024)}, u32[]{:S(2)}) copy-start(s32[2048]{0:T(1024)} %param.8) | copy-start | bytes 24580
  23.9 3.1 %copy-start.2 = (s32[2048]{0:T(1024)S(1)}, s32[2048]{0:T(1024)}, u32[]{:S(2)}) copy-start(s32[2048]{0:T(1024)} %param.7) | copy-start | bytes 24580
  23.9 3.2 %copy-start = (bf16[4,50,800]{2,0,1:T(4,128)(2,1)S(1)}, bf16[4,50,800]{2,0,1:T(4,128)(2,1)}, u32[]{:S(2)}) copy-start(bf16[4,50,800]{2,0,1:T(4,128)(2,1)} %param.6) | copy-start | bytes 960004

commit v6 on v5

--- a/solution.py
+++ b/solution.py
@@ -162,7 +162,7 @@
     for k in range(1, n_x):
         peer = me_z * n_x + lax.rem(me_x + k, n_x)
         for z in range(n_z):
-            first_out[k - 1, z] = one_block((k - 1) * n_z + z)
+            first_out[k - 1, z] = one_block((k - 1) * n_z + z).astype(first_out.dtype)
         pltpu.make_async_remote_copy(
             src_ref=first_out.at[k - 1],
             dst_ref=first_in.at[k - 1],
@@ -182,7 +182,7 @@
             device_id=(me_ab, src),
             device_id_type=MESH,
         ).wait_recv()
-        stage = [stage[z] + first_in[k - 1, z] for z in range(n_z)]
+        stage = [stage[z] + first_in[k - 1, z].astype(jnp.float32) for z in range(n_z)]
 
     for j in range(1, n_z):
         dest_z = lax.rem(me_z + j, n_z)
@@ -190,7 +190,7 @@
         picked = stage[0]
         for z in range(1, n_z):
             picked = jnp.where(dest_z == z, stage[z], picked)
-        second_out[j - 1] = picked
+        second_out[j - 1] = picked.astype(second_out.dtype)
         pltpu.make_async_remote_copy(
             src_ref=second_out.at[j - 1],
             dst_ref=second_in.at[j - 1],
@@ -212,7 +212,7 @@
             device_id=(me_ab, src),
             device_id_type=MESH,
         ).wait_recv()
-        total = total + second_in[j - 1]
+        total = total + second_in[j - 1].astype(jnp.float32)
     out_ref[...] = total.astype(out_ref.dtype)
 
     for k in range(1, n_ab):
@@ -260,10 +260,10 @@
             pltpu.VMEM((n_ab, rows, columns), packed.dtype),
             pltpu.VMEM((width, columns), jnp.float32),
             pltpu.VMEM((n_cd, block, columns), pair_values.dtype),
-            pltpu.VMEM((n_x - 1, n_z, width, block), jnp.float32),
-            pltpu.VMEM((n_x - 1, n_z, width, block), jnp.float32),
-            pltpu.VMEM((n_z - 1, width, block), jnp.float32),
-            pltpu.VMEM((n_z - 1, width, block), jnp.float32),
+            pltpu.VMEM((n_x - 1, n_z, width, block), jnp.bfloat16),
+            pltpu.VMEM((n_x - 1, n_z, width, block), jnp.bfloat16),
+            pltpu.VMEM((n_z - 1, width, block), jnp.bfloat16),
+            pltpu.VMEM((n_z - 1, width, block), jnp.bfloat16),
             pltpu.SemaphoreType.DMA((n_cd,)),
             pltpu.SemaphoreType.DMA((n_ab,)),
             pltpu.SemaphoreType.DMA((n_ab,)),

time: 59.7 us -> 55.6 us (0.931)
  Pallas kernels: 47.5 us -> 43.5 us
    pallas_call x1, Pallas kernels: 29.4 us -> 25.4 us  [ladder(): pl.pallas_call(functools.partial(ladder_kernel, n_ab, n_x, n_z), out_shap...]
where the time goes in v6:
time: 55.6 us; the launch traced here: 55.5 us
  Pallas kernels  43.5 us (78%)
  local copies, waits for them, and re-layouts  7.66 us (14%)
  matrix products  3.43 us (6%)
  between operations  0.81 us (1%)
    pallas_call x1, Pallas kernels, ladder(): pl.pallas_call(functools.partial(ladder_kernel, n_ab, n_x, n_z), out_shap...  25.4 us
    pallas_call x1, Pallas kernels, exchange(): pl.pallas_call(functools.partial(exchange_kernel, n_cd), out_shape=jax.Sh...  18.1 us
    reshape x2, local copies, waits for them, and re-layouts, on_device(): amplitudes.reshape(pair_block, orbit_block, n_cd, orbit_block)  2.99 us
    unnamed x10, local copies, waits for them, and re-layouts  2.47 us
    dot_general x1, matrix products, on_device(): lax.dot_general(mirrored, pick_d.reshape(n_cd, orbit_block, columns), (((...  1.74 us
    dot_general x1, matrix products, on_device(): lax.dot_general(amplitudes, pick_d, (((2,), (0,)), ((), ())), preferred_e...  1.69 us
    reshape x1, local copies, waits for them, and re-layouts, on_device(): landed.reshape(n_cd, padded)[:, :piece]  1.32 us

profile of v6, /device:TPU:2, one launch (start us, length us, event | category | flops | bytes accessed | tf_op | source)
XLA Modules:
  0.0 55.5 jit_solution(9399818708539233384)
XLA Ops:
  0.0 2.5 %reshape.53 = bf16[4,50,16,50]{3,2,0,1:T(8,128)(2,1)S(1)} reshape(bf16[4,50,800]{2,0,1:T(4,128)(2,1)} %param.6) | data formatting | bytes 640000 | tf_op jit(solution)/shard_map/reshape | solution.py:291
  2.5 0.5 copy.19
  3.0 0.8 %reshape.54 = bf16[16,10000]{1,0:T(8,128)(2,1)S(1)} reshape(bf16[16,4,50,50]{3,2,1,0:T(8,128)(2,1)S(1)} %bitcast.43) | data formatting | bytes 640000 | tf_op jit(solution)/shard_map/reshape | solution.py:292
  3.9 0.0 copy-start.1
  3.9 0.8 %copy.13 = bf16[2,8,80,128]{3,2,1,0:T(8,128)(2,1)} copy(bf16[2,8,80,128]{3,1,2,0:T(8,128)(2,1)S(1)} %pad_bitcast_fusion) | data formatting | bytes 655360
  4.7 18.1 %shard_map.55 = bf16[16,80,128]{2,1,0:T(8,128)(2,1)} custom-call(bf16[16,80,128]{2,1,0:T(8,128)(2,1)} %bitcast.44), custom_call_target="tpu_custom_call" | custom-call | tf_op jit(solution)/shard_map/pallas_call | solution.py:77
  22.8 1.1 %copy.20 = bf16[2,8,80,128]{3,1,2,0:T(8,128)(2,1)S(1)} copy(bf16[2,8,80,128]{3,2,1,0:T(8,128)(2,1)} %bitcast.45) | data formatting | bytes 655360
  23.9 0.0 copy-start.2
  23.9 0.0 copy-start
  23.9 1.3 %reshape.57 = bf16[16,4,50,50]{3,2,1,0:T(8,128)(2,1)S(1)} reshape(bf16[16,10000]{1,0:T(8,128)(2,1)S(1)} %slice.4) | data formatting | bytes 640000 | tf_op jit(solution)/shard_map/reshape | solution.py:294
  25.3 0.0 copy-done.1
  25.3 1.7 %fusion.9 = f32[4,50,2048]{2,1,0:T(8,128)S(1)} fusion(bf16[16,4,50,50]{3,2,1,0:T(8,128)(2,1)S(1)} %reshape.57, s32[2048]{0:T(1024)S(1)} %copy-done.1, s32[16,50]{1,0:T(8,128)S(1)} %multiply_add_fusion), kind=kOutput, calls=%fused_computation.9 | convolution fusion | flops 656998400 | bytes 1969792 | tf_op jit(solution)/shard_map/dot_general | solution.py:301
  27.0 0.0 copy-done.2
  27.0 0.1 iota_compare_fusion.1
  27.1 0.0 copy-done
  27.1 1.7 %fusion.21 = f32[4,2048]{1,0:T(4,128)S(1)} fusion(f32[4,50,2048]{2,1,0:T(8,128)S(1)} %fusion.9, s32[2048]{0:T(1024)S(1)} %copy-done.1, pred[50,2048]{1,0:T(8,128)(4,1)S(1)} %iota_compare_fusion.1, bf16[4,50,800]{2,0,1:T(4,128)(2,1)S(1)} %copy-done), kind=kOutput, calls=%fused_computation.13 | convolution fusion | flops 658219008 | bytes 2101760 | tf_op jit(solution)/shard_map/dot_general | solution.py:298
  29.5 25.4 %shard_map.56 = bf16[64,128]{1,0:T(8,128)(2,1)S(1)} custom-call(bf16[4,2048]{1,0:T(4,128)(2,1)S(1)} %multiply_convert_fusion.packed_ref, bf16[2048,2048]{1,0:T(8,128)(2,1)} %values_hbm.1), custom_call_target="tpu_custom_call" | custom-call | tf_op jit(solution)/shard_map/pallas_call | solution.py:254
  54.9 0.6 %copy.23 = bf16[64,128]{1,0:T(8,128)(2,1)} copy(bf16[64,128]{1,0:T(8,128)(2,1)S(1)} %shard_map.56) | data formatting | bytes 32768
  (6 shorter events, 0.1 us)
Async XLA Ops:
  3.9 21.4 %copy-start.1 = (s32[2048]{0:T(1024)S(1)}, s32[2048]{0:T(1024)}, u32[]{:S(2)}) copy-start(s32[2048]{0:T(1024)} %param.8) | copy-start | bytes 24580
  23.9 3.1 %copy-start.2 = (s32[2048]{0:T(1024)S(1)}, s32[2048]{0:T(1024)}, u32[]{:S(2)}) copy-start(s32[2048]{0:T(1024)} %param.7) | copy-start | bytes 24580
  23.9 3.2 %copy-start = (bf16[4,50,800]{2,0,1:T(4,128)(2,1)S(1)}, bf16[4,50,800]{2,0,1:T(4,128)(2,1)}, u32[]{:S(2)}) copy-start(bf16[4,50,800]{2,0,1:T(4,128)(2,1)} %param.6) | copy-start | bytes 960004

commit v7 on v5

--- a/solution.py
+++ b/solution.py
@@ -288,24 +288,22 @@
     pair_block = amplitudes.shape[0]
     piece = pair_block * orbit_block * orbit_block
     padded = -(-piece // 1024) * 1024
-    chunks = jnp.transpose(amplitudes.reshape(pair_block, orbit_block, n_cd, orbit_block), (2, 0, 1, 3))
-    chunks = jnp.pad(chunks.reshape(n_cd, piece), ((0, 0), (0, padded - piece)))
+    rows_first = jnp.transpose(amplitudes, (1, 0, 2)).reshape(orbit_block, pair_block, n_cd, orbit_block)
+    chunks = jnp.transpose(rows_first, (2, 0, 1, 3)).reshape(n_cd, piece)
+    chunks = jnp.pad(chunks, ((0, 0), (0, padded - piece)))
     landed = exchange(chunks.reshape(n_cd, padded // 128, 128), n_cd)
-    mirrored = landed.reshape(n_cd, padded)[:, :piece].reshape(n_cd, pair_block, orbit_block, orbit_block)
+    mirrored = landed.reshape(n_cd, padded)[:, :piece].reshape(n_cd, orbit_block, pair_block, orbit_block)
+    mirrored = jnp.transpose(mirrored, (2, 3, 0, 1)).reshape(pair_block, orbit_block, orbitals)
+    stacked = jnp.concatenate([amplitudes, mirrored], axis=2)
     pick_d = (lax.broadcasted_iota(jnp.int32, (orbitals, columns), 0) == cd_second[None, :]).astype(
         amplitudes.dtype
     )
-    direct_rows = lax.dot_general(
-        amplitudes, pick_d, (((2,), (0,)), ((), ())), preferred_element_type=jnp.float32
-    )
-    crossed_rows = lax.dot_general(
-        mirrored,
-        pick_d.reshape(n_cd, orbit_block, columns),
-        (((0, 2), (0, 1)), ((), ())),
-        preferred_element_type=jnp.float32,
+    pick_twice = jnp.concatenate([pick_d, pick_d], axis=0)
+    both_rows = lax.dot_general(
+        stacked, pick_twice, (((2,), (0,)), ((), ())), preferred_element_type=jnp.float32
     )
     pick_c = lax.broadcasted_iota(jnp.int32, (orbit_block, columns), 0) == local_first[None, :]
-    both = jnp.sum(jnp.where(pick_c[None], direct_rows + crossed_rows, 0.0), axis=1)
+    both = jnp.sum(jnp.where(pick_c[None], both_rows, 0.0), axis=1)
     live_count = live_cols[0]
     slots = jnp.arange(columns, dtype=jnp.int32)
     live = (slots < live_count).astype(jnp.float32)

time: 59.7 us -> 59.9 us (level)
  other arithmetic: 0.09 us -> 1.29 us
  matrix products: 3.43 us -> 2.28 us
    eq x0 -> x1, other arithmetic: none -> 1.21 us  [on_device(): lax.broadcasted_iota(jnp.int32, (orbitals, columns), 0)]
    dot_general x2 -> x1, matrix products: 3.43 us -> 2.28 us  [on_device(): lax.dot_general(stacked, pick_twice, (((2,), (0,)), ((), ())), preferred_...]
    unnamed x10 -> x11, local copies, waits for them, and re-layouts: 2.47 us -> 2.51 us
where the time goes in v7:
time: 59.9 us; the launch traced here: 59.7 us
  Pallas kernels  47.5 us (79%)
  local copies, waits for them, and re-layouts  7.82 us (13%)
  matrix products  2.28 us (4%)
  other arithmetic  1.29 us (2%)
  between operations  0.83 us (1%)
    pallas_call x1, Pallas kernels, ladder(): pl.pallas_call(functools.partial(ladder_kernel, n_ab, n_x, n_z), out_shap...  29.4 us
    pallas_call x1, Pallas kernels, exchange(): pl.pallas_call(functools.partial(exchange_kernel, n_cd), out_shape=jax.Sh...  18.1 us
    unnamed x11, local copies, waits for them, and re-layouts  2.51 us
    reshape x1, local copies, waits for them, and re-layouts, on_device(): jnp.transpose(amplitudes, (1, 0, 2))  2.45 us
    dot_general x1, matrix products, on_device(): lax.dot_general(stacked, pick_twice, (((2,), (0,)), ((), ())), preferred_...  2.28 us
    reshape x1, local copies, waits for them, and re-layouts, on_device(): jnp.transpose(mirrored, (2, 3, 0, 1))  1.24 us
    eq x1, other arithmetic, on_device(): lax.broadcasted_iota(jnp.int32, (orbitals, columns), 0)  1.21 us

profile of v7, /device:TPU:2, one launch (start us, length us, event | category | flops | bytes accessed | tf_op | source)
XLA Modules:
  0.0 59.7 jit_solution(1461496802578359368)
XLA Ops:
  0.0 2.5 %reshape.39 = bf16[50,4,16,50]{3,2,1,0:T(8,128)(2,1)S(1)} reshape(bf16[50,4,800]{2,1,0:T(4,128)(2,1)} %bitcast.23) | data formatting | bytes 640000 | tf_op jit(solution)/shard_map/reshape | solution.py:291
  2.5 0.3 copy.12
  2.8 0.5 reshape.40
  3.3 0.8 %copy.18 = bf16[2,8,80,128]{3,2,1,0:T(8,128)(2,1)} copy(bf16[2,8,80,128]{3,1,2,0:T(8,128)(2,1)S(1)} %pad_bitcast_fusion) | data formatting | bytes 655360
  4.1 18.1 %shard_map.55 = bf16[16,80,128]{2,1,0:T(8,128)(2,1)} custom-call(bf16[16,80,128]{2,1,0:T(8,128)(2,1)} %bitcast.24), custom_call_target="tpu_custom_call" | custom-call | tf_op jit(solution)/shard_map/pallas_call | solution.py:77
  22.2 1.1 %copy.21 = bf16[2,8,80,128]{3,1,2,0:T(8,128)(2,1)S(1)} copy(bf16[2,8,80,128]{3,2,1,0:T(8,128)(2,1)} %bitcast.25) | data formatting | bytes 655360
  23.3 0.0 copy-start.1
  23.3 0.8 %reshape.43 = bf16[16,50,4,50]{3,2,1,0:T(4,128)(2,1)S(1)} reshape(bf16[16,10000]{1,0:T(8,128)(2,1)S(1)} %slice.4) | data formatting | bytes 640000 | tf_op jit(solution)/shard_map/reshape | solution.py:295
  24.1 0.0 copy-start
  24.1 0.0 copy-start.2
  24.1 1.2 %copy.15 = bf16[4,50,800]{2,1,0:T(8,128)(2,1)S(1)} copy(bf16[4,50,800]{1,0,2:T(4,128)(2,1)S(1)} %bitcast.21) | data formatting | bytes 640000 | tf_op jit(solution)/shard_map/reshape | solution.py:296
  25.4 0.0 copy-done.1
  25.4 1.2 %iota_compare_fusion = pred[800,2048]{1,0:T(32,128)(4,1)S(1)} fusion(s32[2048]{0:T(1024)S(1)} %copy-done.1), kind=kLoop, calls=%fused_computation.2 | loop fusion | flops 1638400 | bytes 1646592 | tf_op jit(solution)/shard_map/eq | solution.py:298
  26.6 0.0 copy-done
  26.7 0.0 copy-done.2
  26.7 0.1 iota_compare_fusion.1
  26.8 2.3 %fusion.2 = f32[4,2048]{1,0:T(4,128)S(1)} fusion(pred[800,2048]{1,0:T(32,128)(4,1)S(1)} %iota_compare_fusion, pred[50,2048]{1,0:T(8,128)(4,1)S(1)} %iota_compare_fusion.1, bf16[4,50,800]{2,1,0:T(8,128)(2,1)S(1)} %copy.15, bf16[4,50,800]{2,1,0:T(8,128)(2,1)S(1)} %copy.14), kind=kOutput, calls=%fused_computation.4 | convolution fusion | flops 1316087808 | bytes 2413568 | tf_op jit(solution)/shard_map/dot_general | solution.py:302
  29.7 29.4 %shard_map.56 = bf16[64,128]{1,0:T(8,128)(2,1)S(1)} custom-call(bf16[4,2048]{1,0:T(4,128)(2,1)S(1)} %multiply_convert_fusion.packed_ref, bf16[2048,2048]{1,0:T(8,128)(2,1)} %values_hbm.1), custom_call_target="tpu_custom_call" | custom-call | tf_op jit(solution)/shard_map/pallas_call | solution.py:254
  59.1 0.6 %copy.26 = bf16[64,128]{1,0:T(8,128)(2,1)} copy(bf16[64,128]{1,0:T(8,128)(2,1)S(1)} %shard_map.56) | data formatting | bytes 32768
  (6 shorter events, 0.1 us)
Async XLA Ops:
  23.3 2.1 %copy-start.1 = (s32[2048]{0:T(1024)S(1)}, s32[2048]{0:T(1024)}, u32[]{:S(2)}) copy-start(s32[2048]{0:T(1024)} %param.8) | copy-start | bytes 24580
  24.1 2.5 %copy-start = (bf16[4,50,800]{2,0,1:T(4,128)(2,1)S(1)}, bf16[4,50,800]{2,0,1:T(4,128)(2,1)}, u32[]{:S(2)}) copy-start(bf16[4,50,800]{2,0,1:T(4,128)(2,1)} %param.6) | copy-start | bytes 960004
  24.1 2.6 %copy-start.2 = (s32[2048]{0:T(1024)S(1)}, s32[2048]{0:T(1024)}, u32[]{:S(2)}) copy-start(s32[2048]{0:T(1024)} %param.7) | copy-start | bytes 24580

commit v8 on v5

--- a/solution.py
+++ b/solution.py
@@ -101,9 +101,10 @@
     rows = packed_ref.shape[0]
     block = values_buf.shape[1]
 
+    z_order = [lax.rem(me_z + j, n_z) for j in list(range(1, n_z)) + [0]]
     order = []
-    for k in list(range(1, n_x)) + [0]:
-        for z in range(n_z):
+    for z in z_order:
+        for k in list(range(1, n_x)) + [0]:
             order.append(z * n_x + lax.rem(me_x + k, n_x))
     for step, owner in enumerate(order):
         pltpu.make_async_copy(
@@ -159,60 +160,48 @@
             lhs, values_buf[step], (((1,), (1,)), ((), ())), preferred_element_type=jnp.float32
         )
 
-    for k in range(1, n_x):
-        peer = me_z * n_x + lax.rem(me_x + k, n_x)
-        for z in range(n_z):
-            first_out[k - 1, z] = one_block((k - 1) * n_z + z)
-        pltpu.make_async_remote_copy(
-            src_ref=first_out.at[k - 1],
-            dst_ref=first_in.at[k - 1],
-            send_sem=first_send.at[k - 1],
-            recv_sem=first_recv.at[k - 1],
+    def first_copy(j, k, peer):
+        slot = j * (n_x - 1) + (k - 1)
+        return pltpu.make_async_remote_copy(
+            src_ref=first_out.at[slot],
+            dst_ref=first_in.at[slot],
+            send_sem=first_send.at[slot],
+            recv_sem=first_recv.at[slot],
             device_id=(me_ab, peer),
             device_id_type=MESH,
-        ).start()
-    stage = [one_block((n_x - 1) * n_z + z) for z in range(n_z)]
-    for k in range(1, n_x):
-        src = me_z * n_x + lax.rem(me_x + n_x - k, n_x)
-        pltpu.make_async_remote_copy(
-            src_ref=first_out.at[k - 1],
-            dst_ref=first_in.at[k - 1],
-            send_sem=first_send.at[k - 1],
-            recv_sem=first_recv.at[k - 1],
-            device_id=(me_ab, src),
-            device_id_type=MESH,
-        ).wait_recv()
-        stage = [stage[z] + first_in[k - 1, z] for z in range(n_z)]
-
-    for j in range(1, n_z):
-        dest_z = lax.rem(me_z + j, n_z)
-        peer = dest_z * n_x + me_x
-        picked = stage[0]
-        for z in range(1, n_z):
-            picked = jnp.where(dest_z == z, stage[z], picked)
-        second_out[j - 1] = picked
-        pltpu.make_async_remote_copy(
-            src_ref=second_out.at[j - 1],
-            dst_ref=second_in.at[j - 1],
-            send_sem=second_send.at[j - 1],
-            recv_sem=second_recv.at[j - 1],
+        )
+
+    def second_copy(j, peer):
+        return pltpu.make_async_remote_copy(
+            src_ref=second_out.at[j],
+            dst_ref=second_in.at[j],
+            send_sem=second_send.at[j],
+            recv_sem=second_recv.at[j],
             device_id=(me_ab, peer),
             device_id_type=MESH,
-        ).start()
-    total = stage[0]
-    for z in range(1, n_z):
-        total = jnp.where(me_z == z, stage[z], total)
-    for j in range(1, n_z):
-        src = lax.rem(me_z + n_z - j, n_z) * n_x + me_x
-        pltpu.make_async_remote_copy(
-            src_ref=second_out.at[j - 1],
-            dst_ref=second_in.at[j - 1],
-            send_sem=second_send.at[j - 1],
-            recv_sem=second_recv.at[j - 1],
-            device_id=(me_ab, src),
-            device_id_type=MESH,
-        ).wait_recv()
-        total = total + second_in[j - 1]
+        )
+
+    own = []
+    for j in range(n_z):
+        for k in range(1, n_x):
+            first_out[j * (n_x - 1) + (k - 1)] = one_block(j * n_x + (k - 1))
+            first_copy(j, k, me_z * n_x + lax.rem(me_x + k, n_x)).start()
+        own.append(one_block(j * n_x + (n_x - 1)))
+
+    total = None
+    for j in range(n_z):
+        summed = own[j]
+        for k in range(1, n_x):
+            first_copy(j, k, me_z * n_x + lax.rem(me_x + n_x - k, n_x)).wait_recv()
+            summed = summed + first_in[j * (n_x - 1) + (k - 1)]
+        if j < n_z - 1:
+            second_out[j] = summed
+            second_copy(j, z_order[j] * n_x + me_x).start()
+        else:
+            total = summed
+    for j in range(n_z - 1):
+        second_copy(j, lax.rem(me_z + n_z - 1 - j, n_z) * n_x + me_x).wait_recv()
+        total = total + second_in[j]
     out_ref[...] = total.astype(out_ref.dtype)
 
     for k in range(1, n_ab):
@@ -224,24 +213,11 @@
             device_id=(me_ab, me_cd),
             device_id_type=MESH,
         ).wait_send()
-    for k in range(1, n_x):
-        pltpu.make_async_remote_copy(
-            src_ref=first_out.at[k - 1],
-            dst_ref=first_in.at[k - 1],
-            send_sem=first_send.at[k - 1],
-            recv_sem=first_recv.at[k - 1],
-            device_id=(me_ab, me_cd),
-            device_id_type=MESH,
-        ).wait_send()
-    for j in range(1, n_z):
-        pltpu.make_async_remote_copy(
-            src_ref=second_out.at[j - 1],
-            dst_ref=second_in.at[j - 1],
-            send_sem=second_send.at[j - 1],
-            recv_sem=second_recv.at[j - 1],
-            device_id=(me_ab, me_cd),
-            device_id_type=MESH,
-        ).wait_send()
+    for j in range(n_z):
+        for k in range(1, n_x):
+            first_copy(j, k, me_cd).wait_send()
+    for j in range(n_z - 1):
+        second_copy(j, me_cd).wait_send()
 
 
 def ladder(packed, pair_values, n_ab, n_cd):
@@ -260,15 +236,15 @@
             pltpu.VMEM((n_ab, rows, columns), packed.dtype),
             pltpu.VMEM((width, columns), jnp.float32),
             pltpu.VMEM((n_cd, block, columns), pair_values.dtype),
-            pltpu.VMEM((n_x - 1, n_z, width, block), jnp.float32),
-            pltpu.VMEM((n_x - 1, n_z, width, block), jnp.float32),
+            pltpu.VMEM((n_z * (n_x - 1), width, block), jnp.float32),
+            pltpu.VMEM((n_z * (n_x - 1), width, block), jnp.float32),
             pltpu.VMEM((n_z - 1, width, block), jnp.float32),
             pltpu.VMEM((n_z - 1, width, block), jnp.float32),
             pltpu.SemaphoreType.DMA((n_cd,)),
             pltpu.SemaphoreType.DMA((n_ab,)),
             pltpu.SemaphoreType.DMA((n_ab,)),
-            pltpu.SemaphoreType.DMA((n_x - 1,)),
-            pltpu.SemaphoreType.DMA((n_x - 1,)),
+            pltpu.SemaphoreType.DMA((n_z * (n_x - 1),)),
+            pltpu.SemaphoreType.DMA((n_z * (n_x - 1),)),
             pltpu.SemaphoreType.DMA((n_z - 1,)),
             pltpu.SemaphoreType.DMA((n_z - 1,)),
             pltpu.SemaphoreType.DMA((1,)),

time: 59.7 us -> 54 us (0.905)
  the two profiles are of different devices: /device:TPU:2 before, /device:TPU:1 now
where the time goes in v8:
time: 54 us; the launch traced here: 53.8 us
  Pallas kernels  41.8 us (77%)
  local copies, waits for them, and re-layouts  7.66 us (14%)
  matrix products  3.42 us (6%)
  between operations  0.81 us (2%)
    pallas_call x1, Pallas kernels, ladder(): pl.pallas_call(functools.partial(ladder_kernel, n_ab, n_x, n_z), out_shap...  26 us
    pallas_call x1, Pallas kernels, exchange(): pl.pallas_call(functools.partial(exchange_kernel, n_cd), out_shape=jax.Sh...  15.9 us
    reshape x2, local copies, waits for them, and re-layouts, on_device(): amplitudes.reshape(pair_block, orbit_block, n_cd, orbit_block)  2.99 us
    unnamed x10, local copies, waits for them, and re-layouts  2.47 us
    dot_general x1, matrix products, on_device(): lax.dot_general(mirrored, pick_d.reshape(n_cd, orbit_block, columns), (((...  1.73 us
    dot_general x1, matrix products, on_device(): lax.dot_general(amplitudes, pick_d, (((2,), (0,)), ((), ())), preferred_e...  1.69 us
    reshape x1, local copies, waits for them, and re-layouts, on_device(): landed.reshape(n_cd, padded)[:, :piece]  1.32 us

profile of v8, /device:TPU:1, one launch (start us, length us, event | category | flops | bytes accessed | tf_op | source)
XLA Modules:
  0.0 53.8 jit_solution(2455452058422769036)
XLA Ops:
  0.0 2.5 %reshape.53 = bf16[4,50,16,50]{3,2,0,1:T(8,128)(2,1)S(1)} reshape(bf16[4,50,800]{2,0,1:T(4,128)(2,1)} %param.6) | data formatting | bytes 640000 | tf_op jit(solution)/shard_map/reshape | solution.py:267
  2.5 0.5 %copy.19 = bf16[4,50,16,50]{3,1,0,2:T(8,128)(2,1)S(1)} copy(bf16[4,50,16,50]{3,2,0,1:T(8,128)(2,1)S(1)} %reshape.53) | data formatting | bytes 640000 | tf_op jit(solution)/shard_map/reshape | solution.py:267
  3.0 0.8 %reshape.54 = bf16[16,10000]{1,0:T(8,128)(2,1)S(1)} reshape(bf16[16,4,50,50]{3,2,1,0:T(8,128)(2,1)S(1)} %bitcast.43) | data formatting | bytes 640000 | tf_op jit(solution)/shard_map/reshape | solution.py:268
  3.9 0.0 copy-start.1
  3.9 0.8 %copy.13 = bf16[2,8,80,128]{3,2,1,0:T(8,128)(2,1)} copy(bf16[2,8,80,128]{3,1,2,0:T(8,128)(2,1)S(1)} %pad_bitcast_fusion) | data formatting | bytes 655360
  4.7 15.9 %shard_map.55 = bf16[16,80,128]{2,1,0:T(8,128)(2,1)} custom-call(bf16[16,80,128]{2,1,0:T(8,128)(2,1)} %bitcast.44), custom_call_target="tpu_custom_call" | custom-call | tf_op jit(solution)/shard_map/pallas_call | solution.py:77
  20.5 1.1 %copy.20 = bf16[2,8,80,128]{3,1,2,0:T(8,128)(2,1)S(1)} copy(bf16[2,8,80,128]{3,2,1,0:T(8,128)(2,1)} %bitcast.45) | data formatting | bytes 655360
  21.6 0.0 copy-start.2
  21.6 0.0 copy-start
  21.6 1.3 %reshape.57 = bf16[16,4,50,50]{3,2,1,0:T(8,128)(2,1)S(1)} reshape(bf16[16,10000]{1,0:T(8,128)(2,1)S(1)} %slice.4) | data formatting | bytes 640000 | tf_op jit(solution)/shard_map/reshape | solution.py:270
  23.0 0.0 copy-done.1
  23.0 1.7 %fusion.9 = f32[4,50,2048]{2,1,0:T(8,128)S(1)} fusion(bf16[16,4,50,50]{3,2,1,0:T(8,128)(2,1)S(1)} %reshape.57, s32[2048]{0:T(1024)S(1)} %copy-done.1, s32[16,50]{1,0:T(8,128)S(1)} %multiply_add_fusion), kind=kOutput, calls=%fused_computation.9 | convolution fusion | flops 656998400 | bytes 1969792 | tf_op jit(solution)/shard_map/dot_general | solution.py:277
  24.7 0.0 copy-done.2
  24.8 0.1 iota_compare_fusion.1
  24.8 0.0 copy-done
  24.8 1.7 %fusion.21 = f32[4,2048]{1,0:T(4,128)S(1)} fusion(f32[4,50,2048]{2,1,0:T(8,128)S(1)} %fusion.9, s32[2048]{0:T(1024)S(1)} %copy-done.1, pred[50,2048]{1,0:T(8,128)(4,1)S(1)} %iota_compare_fusion.1, bf16[4,50,800]{2,0,1:T(4,128)(2,1)S(1)} %copy-done), kind=kOutput, calls=%fused_computation.13 | convolution fusion | flops 658219008 | bytes 2101760 | tf_op jit(solution)/shard_map/dot_general | solution.py:274
  27.2 26.0 %shard_map.56 = bf16[64,128]{1,0:T(8,128)(2,1)S(1)} custom-call(bf16[4,2048]{1,0:T(4,128)(2,1)S(1)} %multiply_convert_fusion.packed_ref, bf16[2048,2048]{1,0:T(8,128)(2,1)} %values_hbm.1), custom_call_target="tpu_custom_call" | custom-call | tf_op jit(solution)/shard_map/pallas_call | solution.py:230
  53.2 0.6 %copy.23 = bf16[64,128]{1,0:T(8,128)(2,1)} copy(bf16[64,128]{1,0:T(8,128)(2,1)S(1)} %shard_map.56) | data formatting | bytes 32768
  (6 shorter events, 0.1 us)
Async XLA Ops:
  3.9 19.1 %copy-start.1 = (s32[2048]{0:T(1024)S(1)}, s32[2048]{0:T(1024)}, u32[]{:S(2)}) copy-start(s32[2048]{0:T(1024)} %param.8) | copy-start | bytes 24580
  21.6 3.1 %copy-start.2 = (s32[2048]{0:T(1024)S(1)}, s32[2048]{0:T(1024)}, u32[]{:S(2)}) copy-start(s32[2048]{0:T(1024)} %param.7) | copy-start | bytes 24580
  21.6 3.2 %copy-start = (bf16[4,50,800]{2,0,1:T(4,128)(2,1)S(1)}, bf16[4,50,800]{2,0,1:T(4,128)(2,1)}, u32[]{:S(2)}) copy-start(bf16[4,50,800]{2,0,1:T(4,128)(2,1)} %param.6) | copy-start | bytes 960004

commit v9 on v8

--- a/solution.py
+++ b/solution.py
@@ -264,10 +264,11 @@
     pair_block = amplitudes.shape[0]
     piece = pair_block * orbit_block * orbit_block
     padded = -(-piece // 1024) * 1024
-    chunks = jnp.transpose(amplitudes.reshape(pair_block, orbit_block, n_cd, orbit_block), (2, 0, 1, 3))
-    chunks = jnp.pad(chunks.reshape(n_cd, piece), ((0, 0), (0, padded - piece)))
+    rows_first = jnp.transpose(amplitudes, (1, 0, 2)).reshape(orbit_block, pair_block, n_cd, orbit_block)
+    chunks = jnp.transpose(rows_first, (2, 0, 1, 3)).reshape(n_cd, piece)
+    chunks = jnp.pad(chunks, ((0, 0), (0, padded - piece)))
     landed = exchange(chunks.reshape(n_cd, padded // 128, 128), n_cd)
-    mirrored = landed.reshape(n_cd, padded)[:, :piece].reshape(n_cd, pair_block, orbit_block, orbit_block)
+    mirrored = landed.reshape(n_cd, padded)[:, :piece].reshape(n_cd, orbit_block, pair_block, orbit_block)
     pick_d = (lax.broadcasted_iota(jnp.int32, (orbitals, columns), 0) == cd_second[None, :]).astype(
         amplitudes.dtype
     )
@@ -277,7 +278,7 @@
     crossed_rows = lax.dot_general(
         mirrored,
         pick_d.reshape(n_cd, orbit_block, columns),
-        (((0, 2), (0, 1)), ((), ())),
+        (((0, 1), (0, 1)), ((), ())),
         preferred_element_type=jnp.float32,
     )
     pick_c = lax.broadcasted_iota(jnp.int32, (orbit_block, columns), 0) == local_first[None, :]

time: 54 us -> 52.9 us (0.980)
  local copies, waits for them, and re-layouts: 7.66 us -> 6.53 us
    reshape x3 -> x2, local copies, waits for them, and re-layouts: 3.84 us -> 2.94 us  [the longest x1 2.45 us: on_device(): jnp.transpose(amplitudes, (1, 0, 2))]
where the time goes in v9:
time: 52.9 us; the launch traced here: 52.7 us
  Pallas kernels  41.8 us (79%)
  local copies, waits for them, and re-layouts  6.53 us (12%)
  matrix products  3.47 us (7%)
  between operations  0.81 us (2%)
    pallas_call x1, Pallas kernels, ladder(): pl.pallas_call(functools.partial(ladder_kernel, n_ab, n_x, n_z), out_shap...  26 us
    pallas_call x1, Pallas kernels, exchange(): pl.pallas_call(functools.partial(exchange_kernel, n_cd), out_shape=jax.Sh...  15.9 us
    unnamed x10, local copies, waits for them, and re-layouts  2.47 us
    reshape x1, local copies, waits for them, and re-layouts, on_device(): jnp.transpose(amplitudes, (1, 0, 2))  2.45 us
    dot_general x1, matrix products, on_device(): lax.dot_general(mirrored, pick_d.reshape(n_cd, orbit_block, columns), (((...  1.77 us
    dot_general x1, matrix products, on_device(): lax.dot_general(amplitudes, pick_d, (((2,), (0,)), ((), ())), preferred_e...  1.7 us

profile of v9, /device:TPU:1, one launch (start us, length us, event | category | flops | bytes accessed | tf_op | source)
XLA Modules:
  0.0 52.7 jit_solution(6694874869262500583)
XLA Ops:
  0.0 2.5 %reshape.53 = bf16[50,4,16,50]{3,2,1,0:T(8,128)(2,1)S(1)} reshape(bf16[50,4,800]{2,1,0:T(4,128)(2,1)} %bitcast.42) | data formatting | bytes 640000 | tf_op jit(solution)/shard_map/reshape | solution.py:267
  2.5 0.3 copy.9
  2.8 0.5 reshape.54
  3.3 0.0 copy-start.2
  3.3 0.8 %copy.12 = bf16[2,8,80,128]{3,2,1,0:T(8,128)(2,1)} copy(bf16[2,8,80,128]{3,1,2,0:T(8,128)(2,1)S(1)} %pad_bitcast_fusion) | data formatting | bytes 655360
  4.1 15.9 %shard_map.55 = bf16[16,80,128]{2,1,0:T(8,128)(2,1)} custom-call(bf16[16,80,128]{2,1,0:T(8,128)(2,1)} %bitcast.39), custom_call_target="tpu_custom_call" | custom-call | tf_op jit(solution)/shard_map/pallas_call | solution.py:77
  19.9 1.1 %copy.19 = bf16[2,8,80,128]{3,1,2,0:T(8,128)(2,1)S(1)} copy(bf16[2,8,80,128]{3,2,1,0:T(8,128)(2,1)} %bitcast.40) | data formatting | bytes 655360
  21.0 0.8 %reshape.57 = bf16[16,50,4,50]{3,2,1,0:T(4,128)(2,1)S(1)} reshape(bf16[16,10000]{1,0:T(8,128)(2,1)S(1)} %slice.4) | data formatting | bytes 640000 | tf_op jit(solution)/shard_map/reshape | solution.py:271
  21.8 0.0 copy-done.2
  21.9 0.0 copy-start.1
  21.9 0.0 copy-start
  21.9 1.8 %fusion.9 = f32[4,50,2048]{2,1,0:T(8,128)S(1)} fusion(s32[2048]{0:T(1024)S(1)} %copy-done.2, s32[16,50]{1,0:T(8,128)S(1)} %multiply_add_fusion, bf16[16,50,4,50]{3,2,1,0:T(4,128)(2,1)S(1)} %reshape.57), kind=kOutput, calls=%fused_computation.9 | convolution fusion | flops 656998400 | bytes 1969792 | tf_op jit(solution)/shard_map/dot_general | solution.py:278
  23.7 0.0 copy-done.1
  23.7 0.1 iota_compare_fusion.1
  23.7 0.0 copy-done
  23.8 1.7 %fusion.21 = f32[4,2048]{1,0:T(4,128)S(1)} fusion(f32[4,50,2048]{2,1,0:T(8,128)S(1)} %fusion.9, s32[2048]{0:T(1024)S(1)} %copy-done.2, pred[50,2048]{1,0:T(8,128)(4,1)S(1)} %iota_compare_fusion.1, bf16[4,50,800]{2,0,1:T(4,128)(2,1)S(1)} %copy-done), kind=kOutput, calls=%fused_computation.13 | convolution fusion | flops 658219008 | bytes 2101760 | tf_op jit(solution)/shard_map/dot_general | solution.py:275
  26.1 26.0 %shard_map.56 = bf16[64,128]{1,0:T(8,128)(2,1)S(1)} custom-call(bf16[4,2048]{1,0:T(4,128)(2,1)S(1)} %multiply_convert_fusion.packed_ref, bf16[2048,2048]{1,0:T(8,128)(2,1)} %values_hbm.1), custom_call_target="tpu_custom_call" | custom-call | tf_op jit(solution)/shard_map/pallas_call | solution.py:230
  52.1 0.6 %copy.22 = bf16[64,128]{1,0:T(8,128)(2,1)} copy(bf16[64,128]{1,0:T(8,128)(2,1)S(1)} %shard_map.56) | data formatting | bytes 32768
  (6 shorter events, 0.1 us)
Async XLA Ops:
  3.3 18.5 %copy-start.2 = (s32[2048]{0:T(1024)S(1)}, s32[2048]{0:T(1024)}, u32[]{:S(2)}) copy-start(s32[2048]{0:T(1024)} %param.8) | copy-start | bytes 24580
  21.9 1.8 %copy-start.1 = (s32[2048]{0:T(1024)S(1)}, s32[2048]{0:T(1024)}, u32[]{:S(2)}) copy-start(s32[2048]{0:T(1024)} %param.7) | copy-start | bytes 24580
  21.9 1.9 %copy-start = (bf16[4,50,800]{2,0,1:T(4,128)(2,1)S(1)}, bf16[4,50,800]{2,0,1:T(4,128)(2,1)}, u32[]{:S(2)}) copy-start(bf16[4,50,800]{2,0,1:T(4,128)(2,1)} %param.6) | copy-start | bytes 960004

commit v10 on v9

--- a/solution.py
+++ b/solution.py
@@ -11,7 +11,9 @@
 X_CHIPS = 4
 
 
-def exchange_kernel(n_cd, chunks_ref, out_ref, landed, send_sem, recv_sem, own_sem):
+def exchange_kernel(
+    n_cd, chunks_ref, amp_ref, second_ref, first_ref, out_ref, direct_ref, landed, send_sem, recv_sem, own_sem
+):
     me_ab = lax.axis_index("ab")
     me_cd = lax.axis_index("cd")
     barrier = pltpu.get_barrier_semaphore()
@@ -42,6 +44,13 @@
         def _():
             landed[src] = jnp.zeros(landed.shape[1:], landed.dtype)
 
+    orbitals, columns = amp_ref.shape[2], second_ref.shape[1]
+    pick_d = (lax.broadcasted_iota(jnp.int32, (orbitals, columns), 0) == second_ref[...]).astype(amp_ref.dtype)
+    pick_c = lax.broadcasted_iota(jnp.int32, (amp_ref.shape[1], columns), 0) == first_ref[...]
+    for ij in range(amp_ref.shape[0]):
+        rows = jnp.dot(amp_ref[ij], pick_d, preferred_element_type=jnp.float32)
+        direct_ref[ij:ij + 1, :] = jnp.sum(jnp.where(pick_c, rows, 0.0), axis=0, keepdims=True)
+
     own.wait()
     for k in range(1, n_cd):
         src = lax.rem(me_cd + n_cd - k, n_cd)
@@ -73,12 +82,16 @@
             ).wait_send()
 
 
-def exchange(chunks, n_cd):
+def exchange(chunks, amplitudes, second, local_first, n_cd):
+    pair_block, columns = amplitudes.shape[0], second.shape[0]
     return pl.pallas_call(
         functools.partial(exchange_kernel, n_cd),
-        out_shape=jax.ShapeDtypeStruct(chunks.shape, chunks.dtype),
-        in_specs=[pl.BlockSpec(memory_space=pltpu.VMEM)],
-        out_specs=pl.BlockSpec(memory_space=pltpu.VMEM),
+        out_shape=(
+            jax.ShapeDtypeStruct(chunks.shape, chunks.dtype),
+            jax.ShapeDtypeStruct((pair_block, columns), jnp.float32),
+        ),
+        in_specs=[pl.BlockSpec(memory_space=pltpu.VMEM)] * 4,
+        out_specs=(pl.BlockSpec(memory_space=pltpu.VMEM), pl.BlockSpec(memory_space=pltpu.VMEM)),
         scratch_shapes=[
             pltpu.VMEM(chunks.shape, chunks.dtype),
             pltpu.SemaphoreType.DMA((n_cd,)),
@@ -86,7 +99,7 @@
             pltpu.SemaphoreType.DMA((1,)),
         ],
         compiler_params=pltpu.CompilerParams(collective_id=1, has_side_effects=True),
-    )(chunks)
+    )(chunks, amplitudes, second.reshape(1, columns), local_first.reshape(1, columns))
 
 
 def ladder_kernel(
@@ -267,13 +280,10 @@
     rows_first = jnp.transpose(amplitudes, (1, 0, 2)).reshape(orbit_block, pair_block, n_cd, orbit_block)
     chunks = jnp.transpose(rows_first, (2, 0, 1, 3)).reshape(n_cd, piece)
     chunks = jnp.pad(chunks, ((0, 0), (0, padded - piece)))
-    landed = exchange(chunks.reshape(n_cd, padded // 128, 128), n_cd)
+    landed, direct = exchange(chunks.reshape(n_cd, padded // 128, 128), amplitudes, cd_second, local_first, n_cd)
     mirrored = landed.reshape(n_cd, padded)[:, :piece].reshape(n_cd, orbit_block, pair_block, orbit_block)
     pick_d = (lax.broadcasted_iota(jnp.int32, (orbitals, columns), 0) == cd_second[None, :]).astype(
         amplitudes.dtype
-    )
-    direct_rows = lax.dot_general(
-        amplitudes, pick_d, (((2,), (0,)), ((), ())), preferred_element_type=jnp.float32
     )
     crossed_rows = lax.dot_general(
         mirrored,
@@ -282,7 +292,7 @@
         preferred_element_type=jnp.float32,
     )
     pick_c = lax.broadcasted_iota(jnp.int32, (orbit_block, columns), 0) == local_first[None, :]
-    both = jnp.sum(jnp.where(pick_c[None], direct_rows + crossed_rows, 0.0), axis=1)
+    both = direct + jnp.sum(jnp.where(pick_c[None], crossed_rows, 0.0), axis=1)
     live_count = live_cols[0]
     slots = jnp.arange(columns, dtype=jnp.int32)
     live = (slots < live_count).astype(jnp.float32)

time: 52.9 us -> 52.8 us (level)
  matrix products: 3.47 us -> 1.79 us
  local copies, waits for them, and re-layouts: 6.53 us -> 7.35 us
  other arithmetic: 0.09 us -> 0.69 us
    dot_general x1 -> x0, matrix products: 1.7 us -> none  [on_device(): lax.dot_general(amplitudes, pick_d, (((2,), (0,)), ((), ())), preferred_e...]
    unnamed x10 -> x15, local copies, waits for them, and re-layouts: 2.47 us -> 3.29 us
    sub x1, other arithmetic: 0.01 us -> 0.6 us  [on_device(): local_first = cd_first - slab * orbit_block]
where the time goes in v10:
time: 52.8 us; the launch traced here: 52.6 us
  Pallas kernels  42 us (80%)
  local copies, waits for them, and re-layouts  7.35 us (14%)
  matrix products  1.79 us (3%)
  between operations  0.8 us (2%)
  other arithmetic  0.69 us (1%)
    pallas_call x1, Pallas kernels, ladder(): pl.pallas_call(functools.partial(ladder_kernel, n_ab, n_x, n_z), out_shap...  26 us
    pallas_call x1, Pallas kernels, exchange(): pl.pallas_call(functools.partial(exchange_kernel, n_cd), out_shape=(jax.S...  16 us
    unnamed x15, local copies, waits for them, and re-layouts  3.29 us
    reshape x1, local copies, waits for them, and re-layouts, on_device(): jnp.transpose(amplitudes, (1, 0, 2))  2.45 us
    dot_general x1, matrix products, on_device(): lax.dot_general(mirrored, pick_d.reshape(n_cd, orbit_block, columns), (((...  1.79 us

profile of v10, /device:TPU:1, one launch (start us, length us, event | category | flops | bytes accessed | tf_op | source)
XLA Modules:
  0.0 52.6 jit_solution(5448463823152032370)
XLA Ops:
  0.0 2.5 %reshape.60 = bf16[50,4,16,50]{3,2,1,0:T(8,128)(2,1)S(1)} reshape(bf16[50,4,800]{2,1,0:T(4,128)(2,1)} %bitcast.30) | data formatting | bytes 640000 | tf_op jit(solution)/shard_map/reshape | solution.py:280
  2.5 0.0 copy-start
  2.5 0.3 copy.8
  2.8 0.0 copy-start.3
  2.8 0.5 reshape.61
  3.3 0.8 %copy.12 = bf16[2,8,80,128]{3,2,1,0:T(8,128)(2,1)} copy(bf16[2,8,80,128]{3,1,2,0:T(8,128)(2,1)S(1)} %pad_bitcast_fusion) | data formatting | bytes 655360
  4.1 0.0 copy-done
  4.1 0.8 %copy.9.amp_ref = bf16[4,50,800]{2,1,0:T(8,128)(2,1)} copy(bf16[4,50,800]{2,0,1:T(4,128)(2,1)S(1)} %copy-done) | data formatting | bytes 640000 | tf_op args[1]
  4.9 0.0 copy-start.2
  4.9 0.0 copy-done.3
  4.9 0.6 %broadcast_subtract_fusion = s32[2048]{0:T(1024)} fusion(s32[2048]{0:T(1024)S(1)} %copy-done.3, s32[]{:T(128)S(6)} %mul.14), kind=kLoop, calls=%fused_computation.16 | loop fusion | flops 2048 | bytes 16388 | tf_op jit(solution)/shard_map/sub | solution.py:276
  5.5 0.0 copy-start.1
  5.5 16.0 %shard_map.55 = (bf16[16,80,128]{2,1,0:T(8,128)(2,1)}, f32[4,2048]{1,0:T(4,128)}) custom-call(bf16[16,80,128]{2,1,0:T(8,128)(2,1)} %bitcast.31, bf16[4,50,800]{2,1,0:T(8,128)(2,1)} %copy.9.amp_ref, s32[1,2048]{1,0:T(1,128)} %bitcast.35, s32[1,2048]{1,0:T(1,128)} %bitcast.34), custom_call_target="tpu_custom_call" | custom-call | tf_op jit(solution)/shard_map/pallas_call | solution.py:87
  21.5 1.1 %copy.17 = bf16[2,8,80,128]{3,1,2,0:T(8,128)(2,1)S(1)} copy(bf16[2,8,80,128]{3,2,1,0:T(8,128)(2,1)} %bitcast.33) | data formatting | bytes 655360
  22.6 0.8 %reshape.66 = bf16[16,50,4,50]{3,2,1,0:T(4,128)(2,1)S(1)} reshape(bf16[16,10000]{1,0:T(8,128)(2,1)S(1)} %slice.4) | data formatting | bytes 640000 | tf_op jit(solution)/shard_map/reshape | solution.py:284
  23.4 0.0 copy-done.1
  23.4 0.1 iota_compare_fusion
  23.5 0.0 copy-done.2
  23.5 0.0 copy-start.4
  23.5 1.8 %fusion.11 = f32[4,2048]{1,0:T(4,128)S(1)} fusion(s32[2048]{0:T(1024)S(1)} %copy-done.2, s32[16,50]{1,0:T(8,128)S(1)} %multiply_add_fusion, bf16[16,50,4,50]{3,2,1,0:T(4,128)(2,1)S(1)} %reshape.66, pred[50,2048]{1,0:T(8,128)(4,1)S(1)} %iota_compare_fusion), kind=kOutput, calls=%fused_computation.7 | convolution fusion | flops 657809408 | bytes 466560 | tf_op jit(solution)/shard_map/dot_general | solution.py:288
  26.0 0.0 copy-done.4
  26.0 26.0 %shard_map.56 = bf16[64,128]{1,0:T(8,128)(2,1)S(1)} custom-call(bf16[4,2048]{1,0:T(4,128)(2,1)S(1)} %multiply_convert_fusion.packed_ref, bf16[2048,2048]{1,0:T(8,128)(2,1)} %values_hbm.1), custom_call_target="tpu_custom_call" | custom-call | tf_op jit(solution)/shard_map/pallas_call | solution.py:243
  52.0 0.6 %copy.20 = bf16[64,128]{1,0:T(8,128)(2,1)} copy(bf16[64,128]{1,0:T(8,128)(2,1)S(1)} %shard_map.56) | data formatting | bytes 32768
  (5 shorter events, 0.1 us)
Async XLA Ops:
  2.5 1.7 %copy-start = (bf16[4,50,800]{2,0,1:T(4,128)(2,1)S(1)}, bf16[4,50,800]{2,0,1:T(4,128)(2,1)}, u32[]{:S(2)}) copy-start(bf16[4,50,800]{2,0,1:T(4,128)(2,1)} %param.6) | copy-start | bytes 960004
  2.8 2.1 %copy-start.3 = (s32[2048]{0:T(1024)S(1)}, s32[2048]{0:T(1024)}, u32[]{:S(2)}) copy-start(s32[2048]{0:T(1024)} %param.7) | copy-start | bytes 24580
  4.9 18.6 %copy-start.2 = (s32[2048]{0:T(1024)S(1)}, s32[2048]{0:T(1024)}, u32[]{:S(2)}) copy-start(s32[2048]{0:T(1024)} %param.8) | copy-start | bytes 24580
  5.5 17.9 %copy-start.1 = (s32[2048]{0:T(1024)S(1)}, s32[2048]{0:T(1024)}, u32[]{:S(2)}) copy-start(s32[2048]{0:T(1024)} %broadcast_subtract_fusion) | copy-start | bytes 24580
  23.5 2.5 %copy-start.4 = (f32[4,2048]{1,0:T(4,128)S(1)}, f32[4,2048]{1,0:T(4,128)}, u32[]{:S(2)}) copy-start(f32[4,2048]{1,0:T(4,128)} %get-tuple-element.7) | copy-start | bytes 98308

commit v11 on v10

--- a/solution.py
+++ b/solution.py
@@ -46,7 +46,8 @@
 
     orbitals, columns = amp_ref.shape[2], second_ref.shape[1]
     pick_d = (lax.broadcasted_iota(jnp.int32, (orbitals, columns), 0) == second_ref[...]).astype(amp_ref.dtype)
-    pick_c = lax.broadcasted_iota(jnp.int32, (amp_ref.shape[1], columns), 0) == first_ref[...]
+    local = first_ref[...] - me_cd * amp_ref.shape[1]
+    pick_c = lax.broadcasted_iota(jnp.int32, (amp_ref.shape[1], columns), 0) == local
     for ij in range(amp_ref.shape[0]):
         rows = jnp.dot(amp_ref[ij], pick_d, preferred_element_type=jnp.float32)
         direct_ref[ij:ij + 1, :] = jnp.sum(jnp.where(pick_c, rows, 0.0), axis=0, keepdims=True)
@@ -82,7 +83,7 @@
             ).wait_send()
 
 
-def exchange(chunks, amplitudes, second, local_first, n_cd):
+def exchange(chunks, amplitudes, second, first, n_cd):
     pair_block, columns = amplitudes.shape[0], second.shape[0]
     return pl.pallas_call(
         functools.partial(exchange_kernel, n_cd),
@@ -99,7 +100,7 @@
             pltpu.SemaphoreType.DMA((1,)),
         ],
         compiler_params=pltpu.CompilerParams(collective_id=1, has_side_effects=True),
-    )(chunks, amplitudes, second.reshape(1, columns), local_first.reshape(1, columns))
+    )(chunks, amplitudes, second.reshape(1, columns), first.reshape(1, columns))
 
 
 def ladder_kernel(
@@ -280,7 +281,7 @@
     rows_first = jnp.transpose(amplitudes, (1, 0, 2)).reshape(orbit_block, pair_block, n_cd, orbit_block)
     chunks = jnp.transpose(rows_first, (2, 0, 1, 3)).reshape(n_cd, piece)
     chunks = jnp.pad(chunks, ((0, 0), (0, padded - piece)))
-    landed, direct = exchange(chunks.reshape(n_cd, padded // 128, 128), amplitudes, cd_second, local_first, n_cd)
+    landed, direct = exchange(chunks.reshape(n_cd, padded // 128, 128), amplitudes, cd_second, cd_first, n_cd)
     mirrored = landed.reshape(n_cd, padded)[:, :piece].reshape(n_cd, orbit_block, pair_block, orbit_block)
     pick_d = (lax.broadcasted_iota(jnp.int32, (orbitals, columns), 0) == cd_second[None, :]).astype(
         amplitudes.dtype

time: 52.8 us -> 52.2 us (0.989)
  other arithmetic: 0.69 us -> 0.1 us
    sub x1, other arithmetic: 0.6 us -> 0.01 us  [on_device(): local_first = cd_first - slab * orbit_block]
    unnamed x15 -> x13, local copies, waits for them, and re-layouts: 3.29 us -> 3.28 us
where the time goes in v11:
time: 52.2 us; the launch traced here: 52 us
  Pallas kernels  42 us (80%)
  local copies, waits for them, and re-layouts  7.35 us (14%)
  matrix products  1.8 us (3%)
  between operations  0.8 us (2%)
    pallas_call x1, Pallas kernels, ladder(): pl.pallas_call(functools.partial(ladder_kernel, n_ab, n_x, n_z), out_shap...  26 us
    pallas_call x1, Pallas kernels, exchange(): pl.pallas_call(functools.partial(exchange_kernel, n_cd), out_shape=(jax.S...  16 us
    unnamed x13, local copies, waits for them, and re-layouts  3.28 us
    reshape x1, local copies, waits for them, and re-layouts, on_device(): jnp.transpose(amplitudes, (1, 0, 2))  2.45 us
    dot_general x1, matrix products, on_device(): lax.dot_general(mirrored, pick_d.reshape(n_cd, orbit_block, columns), (((...  1.8 us

profile of v11, /device:TPU:1, one launch (start us, length us, event | category | flops | bytes accessed | tf_op | source)
XLA Modules:
  0.0 52.0 jit_solution(4149639947044329712)
XLA Ops:
  0.0 2.5 %reshape.60 = bf16[50,4,16,50]{3,2,1,0:T(8,128)(2,1)S(1)} reshape(bf16[50,4,800]{2,1,0:T(4,128)(2,1)} %bitcast.30) | data formatting | bytes 640000 | tf_op jit(solution)/shard_map/reshape | solution.py:281
  2.5 0.0 copy-start
  2.5 0.3 copy.8
  2.8 0.5 reshape.61
  3.3 0.8 %copy.12 = bf16[2,8,80,128]{3,2,1,0:T(8,128)(2,1)} copy(bf16[2,8,80,128]{3,1,2,0:T(8,128)(2,1)S(1)} %pad_bitcast_fusion) | data formatting | bytes 655360
  4.1 0.0 copy-done
  4.1 0.0 copy-start.1
  4.1 0.8 %copy.9.amp_ref = bf16[4,50,800]{2,1,0:T(8,128)(2,1)} copy(bf16[4,50,800]{2,0,1:T(4,128)(2,1)S(1)} %copy-done) | data formatting | bytes 640000 | tf_op args[1]
  4.9 0.0 copy-start.2
  4.9 16.0 %shard_map.55 = (bf16[16,80,128]{2,1,0:T(8,128)(2,1)}, f32[4,2048]{1,0:T(4,128)}) custom-call(bf16[16,80,128]{2,1,0:T(8,128)(2,1)} %bitcast.31, bf16[4,50,800]{2,1,0:T(8,128)(2,1)} %copy.9.amp_ref, s32[1,2048]{1,0:T(1,128)} %bitcast.35, s32[1,2048]{1,0:T(1,128)} %bitcast.34), custom_call_target="tpu_custom_call" | custom-call | tf_op jit(solution)/shard_map/pallas_call | solution.py:88
  20.9 1.1 %copy.17 = bf16[2,8,80,128]{3,1,2,0:T(8,128)(2,1)S(1)} copy(bf16[2,8,80,128]{3,2,1,0:T(8,128)(2,1)} %bitcast.33) | data formatting | bytes 655360
  22.0 0.8 %reshape.66 = bf16[16,50,4,50]{3,2,1,0:T(4,128)(2,1)S(1)} reshape(bf16[16,10000]{1,0:T(8,128)(2,1)S(1)} %slice.4) | data formatting | bytes 640000 | tf_op jit(solution)/shard_map/reshape | solution.py:285
  22.8 0.0 copy-done.1
  22.8 0.1 iota_compare_fusion
  22.9 0.0 copy-done.2
  22.9 0.0 copy-start.3
  22.9 1.8 %fusion.11 = f32[4,2048]{1,0:T(4,128)S(1)} fusion(s32[2048]{0:T(1024)S(1)} %copy-done.2, s32[16,50]{1,0:T(8,128)S(1)} %multiply_add_fusion, bf16[16,50,4,50]{3,2,1,0:T(4,128)(2,1)S(1)} %reshape.66, pred[50,2048]{1,0:T(8,128)(4,1)S(1)} %iota_compare_fusion), kind=kOutput, calls=%fused_computation.7 | convolution fusion | flops 657809408 | bytes 466560 | tf_op jit(solution)/shard_map/dot_general | solution.py:289
  25.4 0.0 copy-done.3
  25.4 26.0 %shard_map.56 = bf16[64,128]{1,0:T(8,128)(2,1)S(1)} custom-call(bf16[4,2048]{1,0:T(4,128)(2,1)S(1)} %multiply_convert_fusion.packed_ref, bf16[2048,2048]{1,0:T(8,128)(2,1)} %values_hbm.1), custom_call_target="tpu_custom_call" | custom-call | tf_op jit(solution)/shard_map/pallas_call | solution.py:244
  51.4 0.6 %copy.20 = bf16[64,128]{1,0:T(8,128)(2,1)} copy(bf16[64,128]{1,0:T(8,128)(2,1)S(1)} %shard_map.56) | data formatting | bytes 32768
  (6 shorter events, 0.1 us)
Async XLA Ops:
  2.5 1.6 %copy-start = (bf16[4,50,800]{2,0,1:T(4,128)(2,1)S(1)}, bf16[4,50,800]{2,0,1:T(4,128)(2,1)}, u32[]{:S(2)}) copy-start(bf16[4,50,800]{2,0,1:T(4,128)(2,1)} %param.6) | copy-start | bytes 960004
  4.1 18.7 %copy-start.1 = (s32[2048]{0:T(1024)S(1)}, s32[2048]{0:T(1024)}, u32[]{:S(2)}) copy-start(s32[2048]{0:T(1024)} %param.7) | copy-start | bytes 24580
  4.9 18.0 %copy-start.2 = (s32[2048]{0:T(1024)S(1)}, s32[2048]{0:T(1024)}, u32[]{:S(2)}) copy-start(s32[2048]{0:T(1024)} %param.8) | copy-start | bytes 24580
  22.9 2.5 %copy-start.3 = (f32[4,2048]{1,0:T(4,128)S(1)}, f32[4,2048]{1,0:T(4,128)}, u32[]{:S(2)}) copy-start(f32[4,2048]{1,0:T(4,128)} %get-tuple-element.7) | copy-start | bytes 98308

commit v12 on v11

--- a/solution.py
+++ b/solution.py
@@ -103,6 +103,14 @@
     )(chunks, amplitudes, second.reshape(1, columns), first.reshape(1, columns))
 
 
+def far_first(n):
+    offsets = list(range(1, n))
+    if n % 2 == 0 and n > 2:
+        offsets.remove(n // 2)
+        offsets.insert(0, n // 2)
+    return offsets
+
+
 def ladder_kernel(
     n_ab, n_x, n_z, packed_ref, values_hbm, out_ref,
     slots, gathered, values_buf, first_out, first_in, second_out, second_in,
@@ -115,10 +123,12 @@
     rows = packed_ref.shape[0]
     block = values_buf.shape[1]
 
-    z_order = [lax.rem(me_z + j, n_z) for j in list(range(1, n_z)) + [0]]
+    z_offsets = far_first(n_z)
+    x_offsets = far_first(n_x)
+    z_order = [lax.rem(me_z + o, n_z) for o in z_offsets] + [me_z]
     order = []
     for z in z_order:
-        for k in list(range(1, n_x)) + [0]:
+        for k in x_offsets + [0]:
             order.append(z * n_x + lax.rem(me_x + k, n_x))
     for step, owner in enumerate(order):
         pltpu.make_async_copy(
@@ -197,8 +207,8 @@
 
     own = []
     for j in range(n_z):
-        for k in range(1, n_x):
-            first_out[j * (n_x - 1) + (k - 1)] = one_block(j * n_x + (k - 1))
+        for position, k in enumerate(x_offsets):
+            first_out[j * (n_x - 1) + (k - 1)] = one_block(j * n_x + position)
             first_copy(j, k, me_z * n_x + lax.rem(me_x + k, n_x)).start()
         own.append(one_block(j * n_x + (n_x - 1)))
 
@@ -214,7 +224,7 @@
         else:
             total = summed
     for j in range(n_z - 1):
-        second_copy(j, lax.rem(me_z + n_z - 1 - j, n_z) * n_x + me_x).wait_recv()
+        second_copy(j, lax.rem(me_z + n_z - z_offsets[j], n_z) * n_x + me_x).wait_recv()
         total = total + second_in[j]
     out_ref[...] = total.astype(out_ref.dtype)
 

time: 52.2 us -> 52.3 us (level)
  no operation moved by 1% of the time
where the time goes in v12:
time: 52.3 us; the launch traced here: 52.1 us
  Pallas kernels  42.1 us (80%)
  local copies, waits for them, and re-layouts  7.35 us (14%)
  matrix products  1.8 us (3%)
  between operations  0.8 us (2%)
    pallas_call x1, Pallas kernels, ladder(): pl.pallas_call(functools.partial(ladder_kernel, n_ab, n_x, n_z), out_shap...  26.1 us
    pallas_call x1, Pallas kernels, exchange(): pl.pallas_call(functools.partial(exchange_kernel, n_cd), out_shape=(jax.S...  16 us
    unnamed x13, local copies, waits for them, and re-layouts  3.28 us
    reshape x1, local copies, waits for them, and re-layouts, on_device(): jnp.transpose(amplitudes, (1, 0, 2))  2.45 us
    dot_general x1, matrix products, on_device(): lax.dot_general(mirrored, pick_d.reshape(n_cd, orbit_block, columns), (((...  1.8 us

profile of v12, /device:TPU:1, one launch (start us, length us, event | category | flops | bytes accessed | tf_op | source)
XLA Modules:
  0.0 52.1 jit_solution(15182353310044362652)
XLA Ops:
  0.0 2.5 %reshape.60 = bf16[50,4,16,50]{3,2,1,0:T(8,128)(2,1)S(1)} reshape(bf16[50,4,800]{2,1,0:T(4,128)(2,1)} %bitcast.30) | data formatting | bytes 640000 | tf_op jit(solution)/shard_map/reshape | solution.py:291
  2.5 0.0 copy-start
  2.5 0.3 copy.8
  2.8 0.5 reshape.61
  3.3 0.8 %copy.12 = bf16[2,8,80,128]{3,2,1,0:T(8,128)(2,1)} copy(bf16[2,8,80,128]{3,1,2,0:T(8,128)(2,1)S(1)} %pad_bitcast_fusion) | data formatting | bytes 655360
  4.1 0.0 copy-done
  4.1 0.0 copy-start.1
  4.1 0.8 %copy.9.amp_ref = bf16[4,50,800]{2,1,0:T(8,128)(2,1)} copy(bf16[4,50,800]{2,0,1:T(4,128)(2,1)S(1)} %copy-done) | data formatting | bytes 640000 | tf_op args[1]
  4.9 0.0 copy-start.2
  4.9 16.0 %shard_map.55 = (bf16[16,80,128]{2,1,0:T(8,128)(2,1)}, f32[4,2048]{1,0:T(4,128)}) custom-call(bf16[16,80,128]{2,1,0:T(8,128)(2,1)} %bitcast.31, bf16[4,50,800]{2,1,0:T(8,128)(2,1)} %copy.9.amp_ref, s32[1,2048]{1,0:T(1,128)} %bitcast.35, s32[1,2048]{1,0:T(1,128)} %bitcast.34), custom_call_target="tpu_custom_call" | custom-call | tf_op jit(solution)/shard_map/pallas_call | solution.py:88
  20.9 1.1 %copy.17 = bf16[2,8,80,128]{3,1,2,0:T(8,128)(2,1)S(1)} copy(bf16[2,8,80,128]{3,2,1,0:T(8,128)(2,1)} %bitcast.33) | data formatting | bytes 655360
  22.0 0.8 %reshape.66 = bf16[16,50,4,50]{3,2,1,0:T(4,128)(2,1)S(1)} reshape(bf16[16,10000]{1,0:T(8,128)(2,1)S(1)} %slice.4) | data formatting | bytes 640000 | tf_op jit(solution)/shard_map/reshape | solution.py:295
  22.8 0.0 copy-done.1
  22.8 0.1 iota_compare_fusion
  22.9 0.0 copy-done.2
  22.9 0.0 copy-start.3
  22.9 1.8 %fusion.11 = f32[4,2048]{1,0:T(4,128)S(1)} fusion(s32[2048]{0:T(1024)S(1)} %copy-done.2, s32[16,50]{1,0:T(8,128)S(1)} %multiply_add_fusion, bf16[16,50,4,50]{3,2,1,0:T(4,128)(2,1)S(1)} %reshape.66, pred[50,2048]{1,0:T(8,128)(4,1)S(1)} %iota_compare_fusion), kind=kOutput, calls=%fused_computation.7 | convolution fusion | flops 657809408 | bytes 466560 | tf_op jit(solution)/shard_map/dot_general | solution.py:299
  25.4 0.0 copy-done.3
  25.4 26.1 %shard_map.56 = bf16[64,128]{1,0:T(8,128)(2,1)S(1)} custom-call(bf16[4,2048]{1,0:T(4,128)(2,1)S(1)} %multiply_convert_fusion.packed_ref, bf16[2048,2048]{1,0:T(8,128)(2,1)} %values_hbm.1), custom_call_target="tpu_custom_call" | custom-call | tf_op jit(solution)/shard_map/pallas_call | solution.py:254
  51.5 0.6 %copy.20 = bf16[64,128]{1,0:T(8,128)(2,1)} copy(bf16[64,128]{1,0:T(8,128)(2,1)S(1)} %shard_map.56) | data formatting | bytes 32768
  (6 shorter events, 0.1 us)
Async XLA Ops:
  2.5 1.6 %copy-start = (bf16[4,50,800]{2,0,1:T(4,128)(2,1)S(1)}, bf16[4,50,800]{2,0,1:T(4,128)(2,1)}, u32[]{:S(2)}) copy-start(bf16[4,50,800]{2,0,1:T(4,128)(2,1)} %param.6) | copy-start | bytes 960004
  4.1 18.7 %copy-start.1 = (s32[2048]{0:T(1024)S(1)}, s32[2048]{0:T(1024)}, u32[]{:S(2)}) copy-start(s32[2048]{0:T(1024)} %param.7) | copy-start | bytes 24580
  4.9 18.0 %copy-start.2 = (s32[2048]{0:T(1024)S(1)}, s32[2048]{0:T(1024)}, u32[]{:S(2)}) copy-start(s32[2048]{0:T(1024)} %param.8) | copy-start | bytes 24580
  22.9 2.5 %copy-start.3 = (f32[4,2048]{1,0:T(4,128)S(1)}, f32[4,2048]{1,0:T(4,128)}, u32[]{:S(2)}) copy-start(f32[4,2048]{1,0:T(4,128)} %get-tuple-element.7) | copy-start | bytes 98308

commit v13 on v11

--- a/solution.py
+++ b/solution.py
@@ -120,13 +120,6 @@
     for z in z_order:
         for k in list(range(1, n_x)) + [0]:
             order.append(z * n_x + lax.rem(me_x + k, n_x))
-    for step, owner in enumerate(order):
-        pltpu.make_async_copy(
-            values_hbm.at[pl.ds(pl.multiple_of(owner * block, block), block), :],
-            values_buf.at[step],
-            values_sem.at[step],
-        ).start()
-
     barrier = pltpu.get_barrier_semaphore()
     for k in range(1, n_ab):
         peer = lax.rem(me_ab + k, n_ab)
@@ -150,6 +143,12 @@
             recv_sem=pk_recv.at[me_ab],
             device_id=(peer, me_cd),
             device_id_type=MESH,
+        ).start()
+    for step, owner in enumerate(order):
+        pltpu.make_async_copy(
+            values_hbm.at[pl.ds(pl.multiple_of(owner * block, block), block), :],
+            values_buf.at[step],
+            values_sem.at[step],
         ).start()
     own.wait()
     for k in range(1, n_ab):

time: 52.2 us -> 52.2 us (level)
  no operation moved by 1% of the time
where the time goes in v13:
time: 52.2 us; the launch traced here: 52 us
  Pallas kernels  42 us (80%)
  local copies, waits for them, and re-layouts  7.35 us (14%)
  matrix products  1.8 us (3%)
  between operations  0.8 us (2%)
    pallas_call x1, Pallas kernels, ladder(): pl.pallas_call(functools.partial(ladder_kernel, n_ab, n_x, n_z), out_shap...  26 us
    pallas_call x1, Pallas kernels, exchange(): pl.pallas_call(functools.partial(exchange_kernel, n_cd), out_shape=(jax.S...  16 us
    unnamed x13, local copies, waits for them, and re-layouts  3.28 us
    reshape x1, local copies, waits for them, and re-layouts, on_device(): jnp.transpose(amplitudes, (1, 0, 2))  2.45 us
    dot_general x1, matrix products, on_device(): lax.dot_general(mirrored, pick_d.reshape(n_cd, orbit_block, columns), (((...  1.8 us

profile of v13, /device:TPU:1, one launch (start us, length us, event | category | flops | bytes accessed | tf_op | source)
XLA Modules:
  0.0 52.0 jit_solution(7323917854724191474)
XLA Ops:
  0.0 2.5 %reshape.60 = bf16[50,4,16,50]{3,2,1,0:T(8,128)(2,1)S(1)} reshape(bf16[50,4,800]{2,1,0:T(4,128)(2,1)} %bitcast.30) | data formatting | bytes 640000 | tf_op jit(solution)/shard_map/reshape | solution.py:280
  2.5 0.0 copy-start
  2.5 0.3 copy.8
  2.8 0.5 reshape.61
  3.3 0.8 %copy.12 = bf16[2,8,80,128]{3,2,1,0:T(8,128)(2,1)} copy(bf16[2,8,80,128]{3,1,2,0:T(8,128)(2,1)S(1)} %pad_bitcast_fusion) | data formatting | bytes 655360
  4.1 0.0 copy-done
  4.1 0.0 copy-start.1
  4.1 0.8 %copy.9.amp_ref = bf16[4,50,800]{2,1,0:T(8,128)(2,1)} copy(bf16[4,50,800]{2,0,1:T(4,128)(2,1)S(1)} %copy-done) | data formatting | bytes 640000 | tf_op args[1]
  4.9 0.0 copy-start.2
  4.9 16.0 %shard_map.55 = (bf16[16,80,128]{2,1,0:T(8,128)(2,1)}, f32[4,2048]{1,0:T(4,128)}) custom-call(bf16[16,80,128]{2,1,0:T(8,128)(2,1)} %bitcast.31, bf16[4,50,800]{2,1,0:T(8,128)(2,1)} %copy.9.amp_ref, s32[1,2048]{1,0:T(1,128)} %bitcast.35, s32[1,2048]{1,0:T(1,128)} %bitcast.34), custom_call_target="tpu_custom_call" | custom-call | tf_op jit(solution)/shard_map/pallas_call | solution.py:88
  20.9 1.1 %copy.17 = bf16[2,8,80,128]{3,1,2,0:T(8,128)(2,1)S(1)} copy(bf16[2,8,80,128]{3,2,1,0:T(8,128)(2,1)} %bitcast.33) | data formatting | bytes 655360
  22.0 0.8 %reshape.66 = bf16[16,50,4,50]{3,2,1,0:T(4,128)(2,1)S(1)} reshape(bf16[16,10000]{1,0:T(8,128)(2,1)S(1)} %slice.4) | data formatting | bytes 640000 | tf_op jit(solution)/shard_map/reshape | solution.py:284
  22.8 0.0 copy-done.1
  22.8 0.1 iota_compare_fusion
  22.9 0.0 copy-done.2
  22.9 0.0 copy-start.3
  22.9 1.8 %fusion.11 = f32[4,2048]{1,0:T(4,128)S(1)} fusion(s32[2048]{0:T(1024)S(1)} %copy-done.2, s32[16,50]{1,0:T(8,128)S(1)} %multiply_add_fusion, bf16[16,50,4,50]{3,2,1,0:T(4,128)(2,1)S(1)} %reshape.66, pred[50,2048]{1,0:T(8,128)(4,1)S(1)} %iota_compare_fusion), kind=kOutput, calls=%fused_computation.7 | convolution fusion | flops 657809408 | bytes 466560 | tf_op jit(solution)/shard_map/dot_general | solution.py:288
  25.4 0.0 copy-done.3
  25.4 26.0 %shard_map.56 = bf16[64,128]{1,0:T(8,128)(2,1)S(1)} custom-call(bf16[4,2048]{1,0:T(4,128)(2,1)S(1)} %multiply_convert_fusion.packed_ref, bf16[2048,2048]{1,0:T(8,128)(2,1)} %values_hbm.1), custom_call_target="tpu_custom_call" | custom-call | tf_op jit(solution)/shard_map/pallas_call | solution.py:243
  51.4 0.6 %copy.20 = bf16[64,128]{1,0:T(8,128)(2,1)} copy(bf16[64,128]{1,0:T(8,128)(2,1)S(1)} %shard_map.56) | data formatting | bytes 32768
  (6 shorter events, 0.1 us)
Async XLA Ops:
  2.5 1.6 %copy-start = (bf16[4,50,800]{2,0,1:T(4,128)(2,1)S(1)}, bf16[4,50,800]{2,0,1:T(4,128)(2,1)}, u32[]{:S(2)}) copy-start(bf16[4,50,800]{2,0,1:T(4,128)(2,1)} %param.6) | copy-start | bytes 960004
  4.1 18.7 %copy-start.1 = (s32[2048]{0:T(1024)S(1)}, s32[2048]{0:T(1024)}, u32[]{:S(2)}) copy-start(s32[2048]{0:T(1024)} %param.7) | copy-start | bytes 24580
  4.9 18.0 %copy-start.2 = (s32[2048]{0:T(1024)S(1)}, s32[2048]{0:T(1024)}, u32[]{:S(2)}) copy-start(s32[2048]{0:T(1024)} %param.8) | copy-start | bytes 24580
  22.9 2.5 %copy-start.3 = (f32[4,2048]{1,0:T(4,128)S(1)}, f32[4,2048]{1,0:T(4,128)}, u32[]{:S(2)}) copy-start(f32[4,2048]{1,0:T(4,128)} %get-tuple-element.7) | copy-start | bytes 98308

commit v14 on v13

--- a/solution.py
+++ b/solution.py
@@ -275,13 +275,12 @@
     columns = cd_first.shape[0]
     local_first = cd_first - slab * orbit_block
     pair_block = amplitudes.shape[0]
-    piece = pair_block * orbit_block * orbit_block
-    padded = -(-piece // 1024) * 1024
+    width = 64
     rows_first = jnp.transpose(amplitudes, (1, 0, 2)).reshape(orbit_block, pair_block, n_cd, orbit_block)
-    chunks = jnp.transpose(rows_first, (2, 0, 1, 3)).reshape(n_cd, piece)
-    chunks = jnp.pad(chunks, ((0, 0), (0, padded - piece)))
-    landed, direct = exchange(chunks.reshape(n_cd, padded // 128, 128), amplitudes, cd_second, cd_first, n_cd)
-    mirrored = landed.reshape(n_cd, padded)[:, :piece].reshape(n_cd, orbit_block, pair_block, orbit_block)
+    rows_first = jnp.pad(rows_first, ((0, 0), (0, 0), (0, 0), (0, width - orbit_block)))
+    chunks = jnp.transpose(rows_first, (2, 0, 1, 3)).reshape(n_cd, orbit_block * pair_block * width // 128, 128)
+    landed, direct = exchange(chunks, amplitudes, cd_second, cd_first, n_cd)
+    mirrored = landed.reshape(n_cd, orbit_block, pair_block, width)[..., :orbit_block]
     pick_d = (lax.broadcasted_iota(jnp.int32, (orbitals, columns), 0) == cd_second[None, :]).astype(
         amplitudes.dtype
     )

time: 52.2 us -> 55.3 us (1.059)
  Pallas kernels: 42 us -> 44.6 us
    pallas_call x1, Pallas kernels: 16 us -> 18.8 us  [exchange(): pl.pallas_call(functools.partial(exchange_kernel, n_cd), out_shape=(jax.S...]
    reshape x2, local copies, waits for them, and re-layouts: 1.27 us -> 3.16 us  [the longest x1 1.95 us: on_device(): landed.reshape(n_cd, orbit_block, pair_block, width)[..., :orbit_block]]
    unnamed x13 -> x10, local copies, waits for them, and re-layouts: 3.28 us -> 1.44 us
    reshape x1 -> x2, local copies, waits for them, and re-layouts: 2.45 us -> 2.77 us  [on_device(): jnp.transpose(amplitudes, (1, 0, 2))]
where the time goes in v14:
time: 55.3 us; the launch traced here: 55.2 us
  Pallas kernels  44.6 us (81%)
  local copies, waits for them, and re-layouts  7.8 us (14%)
  matrix products  1.83 us (3%)
  between operations  0.8 us (1%)
    pallas_call x1, Pallas kernels, ladder(): pl.pallas_call(functools.partial(ladder_kernel, n_ab, n_x, n_z), out_shap...  25.8 us
    pallas_call x1, Pallas kernels, exchange(): pl.pallas_call(functools.partial(exchange_kernel, n_cd), out_shape=(jax.S...  18.8 us
    reshape x2, local copies, waits for them, and re-layouts, on_device(): jnp.transpose(amplitudes, (1, 0, 2))  2.77 us
    reshape x1, local copies, waits for them, and re-layouts, on_device(): landed.reshape(n_cd, orbit_block, pair_block, width)[..., :orbit_block]  1.95 us
    dot_general x1, matrix products, on_device(): lax.dot_general(mirrored, pick_d.reshape(n_cd, orbit_block, columns), (((...  1.83 us
    unnamed x10, local copies, waits for them, and re-layouts  1.44 us
    reshape x1, local copies, waits for them, and re-layouts, on_device(): jnp.transpose(rows_first, (2, 0, 1, 3))  1.21 us

profile of v14, /device:TPU:1, one launch (start us, length us, event | category | flops | bytes accessed | tf_op | source)
XLA Modules:
  0.0 55.2 jit_solution(8296226198016936018)
XLA Ops:
  0.0 2.5 %reshape.51 = bf16[50,4,16,50]{3,2,1,0:T(8,128)(2,1)S(1)} reshape(bf16[50,4,800]{2,1,0:T(4,128)(2,1)} %bitcast.24) | data formatting | bytes 640000 | tf_op jit(solution)/shard_map/reshape | solution.py:279
  2.5 0.3 copy.9
  2.8 0.0 copy-start
  2.8 0.4 pad_bitcast_fusion
  3.2 0.0 copy-start.1
  3.3 0.0 copy-start.2
  3.3 1.2 %reshape.52.chunks_ref = bf16[16,100,128]{2,1,0:T(8,128)(2,1)} reshape(bf16[16,50,4,64]{3,2,1,0:T(4,128)(2,1)S(1)} %pad_bitcast_fusion) | data formatting | bytes 819200 | tf_op jit(solution)/shard_map/reshape | solution.py:281
  4.5 0.0 copy-done
  4.5 0.8 %copy.10.amp_ref = bf16[4,50,800]{2,1,0:T(8,128)(2,1)} copy(bf16[4,50,800]{2,0,1:T(4,128)(2,1)S(1)} %copy-done) | data formatting | bytes 640000 | tf_op args[1]
  5.3 18.8 %shard_map.55 = (bf16[16,100,128]{2,1,0:T(8,128)(2,1)}, f32[4,2048]{1,0:T(4,128)}) custom-call(bf16[16,100,128]{2,1,0:T(8,128)(2,1)} %reshape.52.chunks_ref, bf16[4,50,800]{2,1,0:T(8,128)(2,1)} %copy.10.amp_ref, s32[1,2048]{1,0:T(1,128)} %bitcast.27, s32[1,2048]{1,0:T(1,128)} %bitcast.26), custom_call_target="tpu_custom_call" | custom-call | tf_op jit(solution)/shard_map/pallas_call | solution.py:88
  24.1 1.9 %reshape.55 = bf16[16,50,4,64]{3,2,1,0:T(4,128)(2,1)S(1)} reshape(bf16[16,100,128]{2,1,0:T(8,128)(2,1)} %get-tuple-element.8) | data formatting | bytes 819200 | tf_op jit(solution)/shard_map/reshape | solution.py:283
  26.1 0.0 copy-done.1
  26.1 0.1 iota_compare_fusion
  26.2 0.0 copy-done.2
  26.2 0.0 copy-start.3
  26.2 1.8 %fusion.11 = f32[4,2048]{1,0:T(4,128)S(1)} fusion(s32[2048]{0:T(1024)S(1)} %copy-done.2, s32[16,50]{1,0:T(8,128)S(1)} %multiply_add_fusion, bf16[16,50,4,50]{3,2,1,0:T(4,128)(2,1)S(1)} %bitcast.25, pred[50,2048]{1,0:T(8,128)(4,1)S(1)} %iota_compare_fusion), kind=kOutput, calls=%fused_computation.7 | convolution fusion | flops 657809408 | bytes 466560 | tf_op jit(solution)/shard_map/dot_general | solution.py:287
  28.7 0.0 copy-done.3
  28.8 25.8 %shard_map.56 = bf16[64,128]{1,0:T(8,128)(2,1)S(1)} custom-call(bf16[4,2048]{1,0:T(4,128)(2,1)S(1)} %multiply_convert_fusion.packed_ref, bf16[2048,2048]{1,0:T(8,128)(2,1)} %values_hbm.1), custom_call_target="tpu_custom_call" | custom-call | tf_op jit(solution)/shard_map/pallas_call | solution.py:243
  54.6 0.6 %copy.18 = bf16[64,128]{1,0:T(8,128)(2,1)} copy(bf16[64,128]{1,0:T(8,128)(2,1)S(1)} %shard_map.56) | data formatting | bytes 32768
  (4 shorter events, 0.0 us)
Async XLA Ops:
  2.8 1.7 %copy-start = (bf16[4,50,800]{2,0,1:T(4,128)(2,1)S(1)}, bf16[4,50,800]{2,0,1:T(4,128)(2,1)}, u32[]{:S(2)}) copy-start(bf16[4,50,800]{2,0,1:T(4,128)(2,1)} %param.6) | copy-start | bytes 960004
  3.2 22.9 %copy-start.1 = (s32[2048]{0:T(1024)S(1)}, s32[2048]{0:T(1024)}, u32[]{:S(2)}) copy-start(s32[2048]{0:T(1024)} %param.7) | copy-start | bytes 24580
  3.3 23.0 %copy-start.2 = (s32[2048]{0:T(1024)S(1)}, s32[2048]{0:T(1024)}, u32[]{:S(2)}) copy-start(s32[2048]{0:T(1024)} %param.8) | copy-start | bytes 24580
  26.2 2.5 %copy-start.3 = (f32[4,2048]{1,0:T(4,128)S(1)}, f32[4,2048]{1,0:T(4,128)}, u32[]{:S(2)}) copy-start(f32[4,2048]{1,0:T(4,128)} %get-tuple-element.7) | copy-start | bytes 98308

commit v15 on v13

--- a/solution.py
+++ b/solution.py
@@ -12,7 +12,7 @@
 
 
 def exchange_kernel(
-    n_cd, chunks_ref, amp_ref, second_ref, first_ref, out_ref, direct_ref, landed, send_sem, recv_sem, own_sem
+    n_cd, chunks_ref, amp_ref, second_ref, first_ref, landed, direct_ref, send_sem, recv_sem, own_sem
 ):
     me_ab = lax.axis_index("ab")
     me_cd = lax.axis_index("cd")
@@ -67,7 +67,6 @@
                 device_id_type=MESH,
             ).wait_recv()
 
-    out_ref[...] = landed[...]
     for k in range(1, n_cd):
         peer = lax.rem(me_cd + k, n_cd)
 
@@ -94,7 +93,6 @@
         in_specs=[pl.BlockSpec(memory_space=pltpu.VMEM)] * 4,
         out_specs=(pl.BlockSpec(memory_space=pltpu.VMEM), pl.BlockSpec(memory_space=pltpu.VMEM)),
         scratch_shapes=[
-            pltpu.VMEM(chunks.shape, chunks.dtype),
             pltpu.SemaphoreType.DMA((n_cd,)),
             pltpu.SemaphoreType.DMA((n_cd,)),
             pltpu.SemaphoreType.DMA((1,)),

time: 52.2 us -> 52.1 us (level)
  no operation moved by 1% of the time
where the time goes in v15:
time: 52.1 us; the launch traced here: 52 us
  Pallas kernels  41.9 us (80%)
  local copies, waits for them, and re-layouts  7.35 us (14%)
  matrix products  1.8 us (3%)
  between operations  0.8 us (2%)
    pallas_call x1, Pallas kernels, ladder(): pl.pallas_call(functools.partial(ladder_kernel, n_ab, n_x, n_z), out_shap...  26 us
    pallas_call x1, Pallas kernels, exchange(): pl.pallas_call(functools.partial(exchange_kernel, n_cd), out_shape=(jax.S...  16 us
    unnamed x13, local copies, waits for them, and re-layouts  3.28 us
    reshape x1, local copies, waits for them, and re-layouts, on_device(): jnp.transpose(amplitudes, (1, 0, 2))  2.45 us
    dot_general x1, matrix products, on_device(): lax.dot_general(mirrored, pick_d.reshape(n_cd, orbit_block, columns), (((...  1.8 us

profile of v15, /device:TPU:1, one launch (start us, length us, event | category | flops | bytes accessed | tf_op | source)
XLA Modules:
  0.0 52.0 jit_solution(12970140314518534292)
XLA Ops:
  0.0 2.5 %reshape.60 = bf16[50,4,16,50]{3,2,1,0:T(8,128)(2,1)S(1)} reshape(bf16[50,4,800]{2,1,0:T(4,128)(2,1)} %bitcast.30) | data formatting | bytes 640000 | tf_op jit(solution)/shard_map/reshape | solution.py:278
  2.5 0.0 copy-start
  2.5 0.3 copy.8
  2.8 0.5 reshape.61
  3.3 0.8 %copy.12 = bf16[2,8,80,128]{3,2,1,0:T(8,128)(2,1)} copy(bf16[2,8,80,128]{3,1,2,0:T(8,128)(2,1)S(1)} %pad_bitcast_fusion) | data formatting | bytes 655360
  4.1 0.0 copy-done
  4.1 0.0 copy-start.1
  4.1 0.8 %copy.9.amp_ref = bf16[4,50,800]{2,1,0:T(8,128)(2,1)} copy(bf16[4,50,800]{2,0,1:T(4,128)(2,1)S(1)} %copy-done) | data formatting | bytes 640000 | tf_op args[1]
  4.9 0.0 copy-start.2
  4.9 16.0 %shard_map.55 = (bf16[16,80,128]{2,1,0:T(8,128)(2,1)}, f32[4,2048]{1,0:T(4,128)}) custom-call(bf16[16,80,128]{2,1,0:T(8,128)(2,1)} %bitcast.31, bf16[4,50,800]{2,1,0:T(8,128)(2,1)} %copy.9.amp_ref, s32[1,2048]{1,0:T(1,128)} %bitcast.35, s32[1,2048]{1,0:T(1,128)} %bitcast.34), custom_call_target="tpu_custom_call" | custom-call | tf_op jit(solution)/shard_map/pallas_call | solution.py:87
  20.9 1.1 %copy.17 = bf16[2,8,80,128]{3,1,2,0:T(8,128)(2,1)S(1)} copy(bf16[2,8,80,128]{3,2,1,0:T(8,128)(2,1)} %bitcast.33) | data formatting | bytes 655360
  22.0 0.8 %reshape.66 = bf16[16,50,4,50]{3,2,1,0:T(4,128)(2,1)S(1)} reshape(bf16[16,10000]{1,0:T(8,128)(2,1)S(1)} %slice.4) | data formatting | bytes 640000 | tf_op jit(solution)/shard_map/reshape | solution.py:282
  22.8 0.0 copy-done.1
  22.8 0.1 iota_compare_fusion
  22.9 0.0 copy-done.2
  22.9 0.0 copy-start.3
  22.9 1.8 %fusion.11 = f32[4,2048]{1,0:T(4,128)S(1)} fusion(s32[2048]{0:T(1024)S(1)} %copy-done.2, s32[16,50]{1,0:T(8,128)S(1)} %multiply_add_fusion, bf16[16,50,4,50]{3,2,1,0:T(4,128)(2,1)S(1)} %reshape.66, pred[50,2048]{1,0:T(8,128)(4,1)S(1)} %iota_compare_fusion), kind=kOutput, calls=%fused_computation.7 | convolution fusion | flops 657809408 | bytes 466560 | tf_op jit(solution)/shard_map/dot_general | solution.py:286
  25.4 0.0 copy-done.3
  25.4 26.0 %shard_map.56 = bf16[64,128]{1,0:T(8,128)(2,1)S(1)} custom-call(bf16[4,2048]{1,0:T(4,128)(2,1)S(1)} %multiply_convert_fusion.packed_ref, bf16[2048,2048]{1,0:T(8,128)(2,1)} %values_hbm.1), custom_call_target="tpu_custom_call" | custom-call | tf_op jit(solution)/shard_map/pallas_call | solution.py:241
  51.4 0.6 %copy.20 = bf16[64,128]{1,0:T(8,128)(2,1)} copy(bf16[64,128]{1,0:T(8,128)(2,1)S(1)} %shard_map.56) | data formatting | bytes 32768
  (6 shorter events, 0.1 us)
Async XLA Ops:
  2.5 1.6 %copy-start = (bf16[4,50,800]{2,0,1:T(4,128)(2,1)S(1)}, bf16[4,50,800]{2,0,1:T(4,128)(2,1)}, u32[]{:S(2)}) copy-start(bf16[4,50,800]{2,0,1:T(4,128)(2,1)} %param.6) | copy-start | bytes 960004
  4.1 18.7 %copy-start.1 = (s32[2048]{0:T(1024)S(1)}, s32[2048]{0:T(1024)}, u32[]{:S(2)}) copy-start(s32[2048]{0:T(1024)} %param.7) | copy-start | bytes 24580
  4.9 18.0 %copy-start.2 = (s32[2048]{0:T(1024)S(1)}, s32[2048]{0:T(1024)}, u32[]{:S(2)}) copy-start(s32[2048]{0:T(1024)} %param.8) | copy-start | bytes 24580
  22.9 2.5 %copy-start.3 = (f32[4,2048]{1,0:T(4,128)S(1)}, f32[4,2048]{1,0:T(4,128)}, u32[]{:S(2)}) copy-start(f32[4,2048]{1,0:T(4,128)} %get-tuple-element.7) | copy-start | bytes 98308

commit v16 on v15

--- a/solution.py
+++ b/solution.py
@@ -160,8 +160,8 @@
             device_id_type=MESH,
         ).wait_recv()
     for k in range(n_ab):
-        gathered[k * rows:(k + 1) * rows, :] = slots[k].astype(jnp.float32)
-    lhs = gathered[...].astype(jnp.bfloat16)
+        gathered[k * rows:(k + 1) * rows, :] = slots[k]
+    lhs = gathered[...]
 
     def one_block(step):
         pltpu.make_async_copy(
@@ -245,7 +245,7 @@
         out_specs=pl.BlockSpec(memory_space=pltpu.VMEM),
         scratch_shapes=[
             pltpu.VMEM((n_ab, rows, columns), packed.dtype),
-            pltpu.VMEM((width, columns), jnp.float32),
+            pltpu.VMEM((width, columns), packed.dtype),
             pltpu.VMEM((n_cd, block, columns), pair_values.dtype),
             pltpu.VMEM((n_z * (n_x - 1), width, block), jnp.float32),
             pltpu.VMEM((n_z * (n_x - 1), width, block), jnp.float32),

time: 52.1 us -> 52.1 us (level)
  no operation moved by 1% of the time
where the time goes in v16:
time: 52.1 us; the launch traced here: 52 us
  Pallas kernels  41.9 us (80%)
  local copies, waits for them, and re-layouts  7.35 us (14%)
  matrix products  1.8 us (3%)
  between operations  0.8 us (2%)
    pallas_call x1, Pallas kernels, ladder(): pl.pallas_call(functools.partial(ladder_kernel, n_ab, n_x, n_z), out_shap...  25.9 us
    pallas_call x1, Pallas kernels, exchange(): pl.pallas_call(functools.partial(exchange_kernel, n_cd), out_shape=(jax.S...  16 us
    unnamed x13, local copies, waits for them, and re-layouts  3.28 us
    reshape x1, local copies, waits for them, and re-layouts, on_device(): jnp.transpose(amplitudes, (1, 0, 2))  2.45 us
    dot_general x1, matrix products, on_device(): lax.dot_general(mirrored, pick_d.reshape(n_cd, orbit_block, columns), (((...  1.8 us

profile of v16, /device:TPU:1, one launch (start us, length us, event | category | flops | bytes accessed | tf_op | source)
XLA Modules:
  0.0 52.0 jit_solution(18133440110368539231)
XLA Ops:
  0.0 2.5 %reshape.60 = bf16[50,4,16,50]{3,2,1,0:T(8,128)(2,1)S(1)} reshape(bf16[50,4,800]{2,1,0:T(4,128)(2,1)} %bitcast.30) | data formatting | bytes 640000 | tf_op jit(solution)/shard_map/reshape | solution.py:278
  2.5 0.0 copy-start
  2.5 0.3 copy.8
  2.8 0.5 reshape.61
  3.3 0.8 %copy.12 = bf16[2,8,80,128]{3,2,1,0:T(8,128)(2,1)} copy(bf16[2,8,80,128]{3,1,2,0:T(8,128)(2,1)S(1)} %pad_bitcast_fusion) | data formatting | bytes 655360
  4.1 0.0 copy-done
  4.1 0.0 copy-start.1
  4.1 0.8 %copy.9.amp_ref = bf16[4,50,800]{2,1,0:T(8,128)(2,1)} copy(bf16[4,50,800]{2,0,1:T(4,128)(2,1)S(1)} %copy-done) | data formatting | bytes 640000 | tf_op args[1]
  4.9 0.0 copy-start.2
  4.9 16.0 %shard_map.55 = (bf16[16,80,128]{2,1,0:T(8,128)(2,1)}, f32[4,2048]{1,0:T(4,128)}) custom-call(bf16[16,80,128]{2,1,0:T(8,128)(2,1)} %bitcast.31, bf16[4,50,800]{2,1,0:T(8,128)(2,1)} %copy.9.amp_ref, s32[1,2048]{1,0:T(1,128)} %bitcast.35, s32[1,2048]{1,0:T(1,128)} %bitcast.34), custom_call_target="tpu_custom_call" | custom-call | tf_op jit(solution)/shard_map/pallas_call | solution.py:87
  20.9 1.1 %copy.17 = bf16[2,8,80,128]{3,1,2,0:T(8,128)(2,1)S(1)} copy(bf16[2,8,80,128]{3,2,1,0:T(8,128)(2,1)} %bitcast.33) | data formatting | bytes 655360
  22.0 0.8 %reshape.66 = bf16[16,50,4,50]{3,2,1,0:T(4,128)(2,1)S(1)} reshape(bf16[16,10000]{1,0:T(8,128)(2,1)S(1)} %slice.4) | data formatting | bytes 640000 | tf_op jit(solution)/shard_map/reshape | solution.py:282
  22.8 0.0 copy-done.1
  22.8 0.1 iota_compare_fusion
  22.9 0.0 copy-done.2
  22.9 0.0 copy-start.3
  22.9 1.8 %fusion.11 = f32[4,2048]{1,0:T(4,128)S(1)} fusion(s32[2048]{0:T(1024)S(1)} %copy-done.2, s32[16,50]{1,0:T(8,128)S(1)} %multiply_add_fusion, bf16[16,50,4,50]{3,2,1,0:T(4,128)(2,1)S(1)} %reshape.66, pred[50,2048]{1,0:T(8,128)(4,1)S(1)} %iota_compare_fusion), kind=kOutput, calls=%fused_computation.7 | convolution fusion | flops 657809408 | bytes 466560 | tf_op jit(solution)/shard_map/dot_general | solution.py:286
  25.4 0.0 copy-done.3
  25.4 25.9 %shard_map.56 = bf16[64,128]{1,0:T(8,128)(2,1)S(1)} custom-call(bf16[4,2048]{1,0:T(4,128)(2,1)S(1)} %multiply_convert_fusion.packed_ref, bf16[2048,2048]{1,0:T(8,128)(2,1)} %values_hbm.1), custom_call_target="tpu_custom_call" | custom-call | tf_op jit(solution)/shard_map/pallas_call | solution.py:241
  51.3 0.6 %copy.20 = bf16[64,128]{1,0:T(8,128)(2,1)} copy(bf16[64,128]{1,0:T(8,128)(2,1)S(1)} %shard_map.56) | data formatting | bytes 32768
  (6 shorter events, 0.1 us)
Async XLA Ops:
  2.5 1.6 %copy-start = (bf16[4,50,800]{2,0,1:T(4,128)(2,1)S(1)}, bf16[4,50,800]{2,0,1:T(4,128)(2,1)}, u32[]{:S(2)}) copy-start(bf16[4,50,800]{2,0,1:T(4,128)(2,1)} %param.6) | copy-start | bytes 960004
  4.1 18.7 %copy-start.1 = (s32[2048]{0:T(1024)S(1)}, s32[2048]{0:T(1024)}, u32[]{:S(2)}) copy-start(s32[2048]{0:T(1024)} %param.7) | copy-start | bytes 24580
  4.9 18.0 %copy-start.2 = (s32[2048]{0:T(1024)S(1)}, s32[2048]{0:T(1024)}, u32[]{:S(2)}) copy-start(s32[2048]{0:T(1024)} %param.8) | copy-start | bytes 24580
  22.9 2.5 %copy-start.3 = (f32[4,2048]{1,0:T(4,128)S(1)}, f32[4,2048]{1,0:T(4,128)}, u32[]{:S(2)}) copy-start(f32[4,2048]{1,0:T(4,128)} %get-tuple-element.7) | copy-start | bytes 98308

commit v17 on v15

--- a/solution.py
+++ b/solution.py
@@ -24,7 +24,7 @@
     own = pltpu.make_async_copy(chunks_ref.at[me_cd], landed.at[me_cd], own_sem.at[0])
     own.start()
     for k in range(1, n_cd):
-        peer = lax.rem(me_cd + k, n_cd)
+        peer = lax.rem(me_cd + n_cd - k, n_cd)
 
         @pl.when(peer < me_cd)
         def _():
@@ -68,7 +68,7 @@
             ).wait_recv()
 
     for k in range(1, n_cd):
-        peer = lax.rem(me_cd + k, n_cd)
+        peer = lax.rem(me_cd + n_cd - k, n_cd)
 
         @pl.when(peer < me_cd)
         def _():

time: 52.1 us -> 53.7 us (1.031)
  Pallas kernels: 41.9 us -> 43.5 us
    pallas_call x1, Pallas kernels: 16 us -> 18.6 us  [exchange(): pl.pallas_call(functools.partial(exchange_kernel, n_cd), out_shape=(jax.S...]
    pallas_call x1, Pallas kernels: 26 us -> 24.9 us  [ladder(): pl.pallas_call(functools.partial(ladder_kernel, n_ab, n_x, n_z), out_shap...]
where the time goes in v17:
time: 53.7 us; the launch traced here: 53.5 us
  Pallas kernels  43.5 us (81%)
  local copies, waits for them, and re-layouts  7.35 us (14%)
  matrix products  1.79 us (3%)
  between operations  0.8 us (1%)
    pallas_call x1, Pallas kernels, ladder(): pl.pallas_call(functools.partial(ladder_kernel, n_ab, n_x, n_z), out_shap...  24.9 us
    pallas_call x1, Pallas kernels, exchange(): pl.pallas_call(functools.partial(exchange_kernel, n_cd), out_shape=(jax.S...  18.6 us
    unnamed x13, local copies, waits for them, and re-layouts  3.28 us
    reshape x1, local copies, waits for them, and re-layouts, on_device(): jnp.transpose(amplitudes, (1, 0, 2))  2.45 us
    dot_general x1, matrix products, on_device(): lax.dot_general(mirrored, pick_d.reshape(n_cd, orbit_block, columns), (((...  1.79 us

profile of v17, /device:TPU:1, one launch (start us, length us, event | category | flops | bytes accessed | tf_op | source)
XLA Modules:
  0.0 53.5 jit_solution(12195637095650498812)
XLA Ops:
  0.0 2.5 %reshape.60 = bf16[50,4,16,50]{3,2,1,0:T(8,128)(2,1)S(1)} reshape(bf16[50,4,800]{2,1,0:T(4,128)(2,1)} %bitcast.30) | data formatting | bytes 640000 | tf_op jit(solution)/shard_map/reshape | solution.py:278
  2.5 0.0 copy-start
  2.5 0.3 copy.8
  2.8 0.5 reshape.61
  3.3 0.8 %copy.12 = bf16[2,8,80,128]{3,2,1,0:T(8,128)(2,1)} copy(bf16[2,8,80,128]{3,1,2,0:T(8,128)(2,1)S(1)} %pad_bitcast_fusion) | data formatting | bytes 655360
  4.1 0.0 copy-done
  4.1 0.0 copy-start.1
  4.1 0.8 %copy.9.amp_ref = bf16[4,50,800]{2,1,0:T(8,128)(2,1)} copy(bf16[4,50,800]{2,0,1:T(4,128)(2,1)S(1)} %copy-done) | data formatting | bytes 640000 | tf_op args[1]
  4.9 0.0 copy-start.2
  4.9 18.6 %shard_map.55 = (bf16[16,80,128]{2,1,0:T(8,128)(2,1)}, f32[4,2048]{1,0:T(4,128)}) custom-call(bf16[16,80,128]{2,1,0:T(8,128)(2,1)} %bitcast.31, bf16[4,50,800]{2,1,0:T(8,128)(2,1)} %copy.9.amp_ref, s32[1,2048]{1,0:T(1,128)} %bitcast.35, s32[1,2048]{1,0:T(1,128)} %bitcast.34), custom_call_target="tpu_custom_call" | custom-call | tf_op jit(solution)/shard_map/pallas_call | solution.py:87
  23.5 1.1 %copy.17 = bf16[2,8,80,128]{3,1,2,0:T(8,128)(2,1)S(1)} copy(bf16[2,8,80,128]{3,2,1,0:T(8,128)(2,1)} %bitcast.33) | data formatting | bytes 655360
  24.6 0.8 %reshape.66 = bf16[16,50,4,50]{3,2,1,0:T(4,128)(2,1)S(1)} reshape(bf16[16,10000]{1,0:T(8,128)(2,1)S(1)} %slice.4) | data formatting | bytes 640000 | tf_op jit(solution)/shard_map/reshape | solution.py:282
  25.4 0.0 copy-done.1
  25.4 0.1 iota_compare_fusion
  25.5 0.0 copy-done.2
  25.5 0.0 copy-start.3
  25.5 1.8 %fusion.11 = f32[4,2048]{1,0:T(4,128)S(1)} fusion(s32[2048]{0:T(1024)S(1)} %copy-done.2, s32[16,50]{1,0:T(8,128)S(1)} %multiply_add_fusion, bf16[16,50,4,50]{3,2,1,0:T(4,128)(2,1)S(1)} %reshape.66, pred[50,2048]{1,0:T(8,128)(4,1)S(1)} %iota_compare_fusion), kind=kOutput, calls=%fused_computation.7 | convolution fusion | flops 657809408 | bytes 466560 | tf_op jit(solution)/shard_map/dot_general | solution.py:286
  28.0 0.0 copy-done.3
  28.0 24.9 %shard_map.56 = bf16[64,128]{1,0:T(8,128)(2,1)S(1)} custom-call(bf16[4,2048]{1,0:T(4,128)(2,1)S(1)} %multiply_convert_fusion.packed_ref, bf16[2048,2048]{1,0:T(8,128)(2,1)} %values_hbm.1), custom_call_target="tpu_custom_call" | custom-call | tf_op jit(solution)/shard_map/pallas_call | solution.py:241
  52.9 0.6 %copy.20 = bf16[64,128]{1,0:T(8,128)(2,1)} copy(bf16[64,128]{1,0:T(8,128)(2,1)S(1)} %shard_map.56) | data formatting | bytes 32768
  (6 shorter events, 0.1 us)
Async XLA Ops:
  2.5 1.6 %copy-start = (bf16[4,50,800]{2,0,1:T(4,128)(2,1)S(1)}, bf16[4,50,800]{2,0,1:T(4,128)(2,1)}, u32[]{:S(2)}) copy-start(bf16[4,50,800]{2,0,1:T(4,128)(2,1)} %param.6) | copy-start | bytes 960004
  4.1 21.3 %copy-start.1 = (s32[2048]{0:T(1024)S(1)}, s32[2048]{0:T(1024)}, u32[]{:S(2)}) copy-start(s32[2048]{0:T(1024)} %param.7) | copy-start | bytes 24580
  4.9 20.6 %copy-start.2 = (s32[2048]{0:T(1024)S(1)}, s32[2048]{0:T(1024)}, u32[]{:S(2)}) copy-start(s32[2048]{0:T(1024)} %param.8) | copy-start | bytes 24580
  25.5 2.5 %copy-start.3 = (f32[4,2048]{1,0:T(4,128)S(1)}, f32[4,2048]{1,0:T(4,128)}, u32[]{:S(2)}) copy-start(f32[4,2048]{1,0:T(4,128)} %get-tuple-element.7) | copy-start | bytes 98308

commit v18 on v15

--- a/solution.py
+++ b/solution.py
@@ -22,7 +22,6 @@
         pl.semaphore_signal(barrier, inc=1, device_id=(me_ab, peer), device_id_type=MESH)
     pl.semaphore_wait(barrier, n_cd - 1)
     own = pltpu.make_async_copy(chunks_ref.at[me_cd], landed.at[me_cd], own_sem.at[0])
-    own.start()
     for k in range(1, n_cd):
         peer = lax.rem(me_cd + k, n_cd)
 
@@ -37,6 +36,7 @@
                 device_id_type=MESH,
             ).start()
 
+    own.start()
     for k in range(1, n_cd):
         src = lax.rem(me_cd + k, n_cd)
 

time: 52.1 us -> 52.1 us (level)
  no operation moved by 1% of the time
where the time goes in v18:
time: 52.1 us; the launch traced here: 52 us
  Pallas kernels  41.9 us (80%)
  local copies, waits for them, and re-layouts  7.35 us (14%)
  matrix products  1.81 us (3%)
  between operations  0.8 us (2%)
    pallas_call x1, Pallas kernels, ladder(): pl.pallas_call(functools.partial(ladder_kernel, n_ab, n_x, n_z), out_shap...  25.9 us
    pallas_call x1, Pallas kernels, exchange(): pl.pallas_call(functools.partial(exchange_kernel, n_cd), out_shape=(jax.S...  16 us
    unnamed x13, local copies, waits for them, and re-layouts  3.28 us
    reshape x1, local copies, waits for them, and re-layouts, on_device(): jnp.transpose(amplitudes, (1, 0, 2))  2.45 us
    dot_general x1, matrix products, on_device(): lax.dot_general(mirrored, pick_d.reshape(n_cd, orbit_block, columns), (((...  1.81 us

profile of v18, /device:TPU:1, one launch (start us, length us, event | category | flops | bytes accessed | tf_op | source)
XLA Modules:
  0.0 52.0 jit_solution(8709553719699324999)
XLA Ops:
  0.0 2.5 %reshape.60 = bf16[50,4,16,50]{3,2,1,0:T(8,128)(2,1)S(1)} reshape(bf16[50,4,800]{2,1,0:T(4,128)(2,1)} %bitcast.30) | data formatting | bytes 640000 | tf_op jit(solution)/shard_map/reshape | solution.py:278
  2.5 0.0 copy-start
  2.5 0.3 copy.8
  2.8 0.5 reshape.61
  3.3 0.8 %copy.12 = bf16[2,8,80,128]{3,2,1,0:T(8,128)(2,1)} copy(bf16[2,8,80,128]{3,1,2,0:T(8,128)(2,1)S(1)} %pad_bitcast_fusion) | data formatting | bytes 655360
  4.1 0.0 copy-done
  4.1 0.0 copy-start.1
  4.1 0.8 %copy.9.amp_ref = bf16[4,50,800]{2,1,0:T(8,128)(2,1)} copy(bf16[4,50,800]{2,0,1:T(4,128)(2,1)S(1)} %copy-done) | data formatting | bytes 640000 | tf_op args[1]
  4.9 0.0 copy-start.2
  4.9 16.0 %shard_map.55 = (bf16[16,80,128]{2,1,0:T(8,128)(2,1)}, f32[4,2048]{1,0:T(4,128)}) custom-call(bf16[16,80,128]{2,1,0:T(8,128)(2,1)} %bitcast.31, bf16[4,50,800]{2,1,0:T(8,128)(2,1)} %copy.9.amp_ref, s32[1,2048]{1,0:T(1,128)} %bitcast.35, s32[1,2048]{1,0:T(1,128)} %bitcast.34), custom_call_target="tpu_custom_call" | custom-call | tf_op jit(solution)/shard_map/pallas_call | solution.py:87
  20.9 1.1 %copy.17 = bf16[2,8,80,128]{3,1,2,0:T(8,128)(2,1)S(1)} copy(bf16[2,8,80,128]{3,2,1,0:T(8,128)(2,1)} %bitcast.33) | data formatting | bytes 655360
  22.0 0.8 %reshape.66 = bf16[16,50,4,50]{3,2,1,0:T(4,128)(2,1)S(1)} reshape(bf16[16,10000]{1,0:T(8,128)(2,1)S(1)} %slice.4) | data formatting | bytes 640000 | tf_op jit(solution)/shard_map/reshape | solution.py:282
  22.8 0.0 copy-done.1
  22.8 0.1 iota_compare_fusion
  22.9 0.0 copy-done.2
  22.9 0.0 copy-start.3
  22.9 1.8 %fusion.11 = f32[4,2048]{1,0:T(4,128)S(1)} fusion(s32[2048]{0:T(1024)S(1)} %copy-done.2, s32[16,50]{1,0:T(8,128)S(1)} %multiply_add_fusion, bf16[16,50,4,50]{3,2,1,0:T(4,128)(2,1)S(1)} %reshape.66, pred[50,2048]{1,0:T(8,128)(4,1)S(1)} %iota_compare_fusion), kind=kOutput, calls=%fused_computation.7 | convolution fusion | flops 657809408 | bytes 466560 | tf_op jit(solution)/shard_map/dot_general | solution.py:286
  25.4 0.0 copy-done.3
  25.4 25.9 %shard_map.56 = bf16[64,128]{1,0:T(8,128)(2,1)S(1)} custom-call(bf16[4,2048]{1,0:T(4,128)(2,1)S(1)} %multiply_convert_fusion.packed_ref, bf16[2048,2048]{1,0:T(8,128)(2,1)} %values_hbm.1), custom_call_target="tpu_custom_call" | custom-call | tf_op jit(solution)/shard_map/pallas_call | solution.py:241
  51.4 0.6 %copy.20 = bf16[64,128]{1,0:T(8,128)(2,1)} copy(bf16[64,128]{1,0:T(8,128)(2,1)S(1)} %shard_map.56) | data formatting | bytes 32768
  (6 shorter events, 0.1 us)
Async XLA Ops:
  2.5 1.6 %copy-start = (bf16[4,50,800]{2,0,1:T(4,128)(2,1)S(1)}, bf16[4,50,800]{2,0,1:T(4,128)(2,1)}, u32[]{:S(2)}) copy-start(bf16[4,50,800]{2,0,1:T(4,128)(2,1)} %param.6) | copy-start | bytes 960004
  4.1 18.7 %copy-start.1 = (s32[2048]{0:T(1024)S(1)}, s32[2048]{0:T(1024)}, u32[]{:S(2)}) copy-start(s32[2048]{0:T(1024)} %param.7) | copy-start | bytes 24580
  4.9 18.0 %copy-start.2 = (s32[2048]{0:T(1024)S(1)}, s32[2048]{0:T(1024)}, u32[]{:S(2)}) copy-start(s32[2048]{0:T(1024)} %param.8) | copy-start | bytes 24580
  22.9 2.5 %copy-start.3 = (f32[4,2048]{1,0:T(4,128)S(1)}, f32[4,2048]{1,0:T(4,128)}, u32[]{:S(2)}) copy-start(f32[4,2048]{1,0:T(4,128)} %get-tuple-element.7) | copy-start | bytes 98308

commit v19 on v15

--- a/solution.py
+++ b/solution.py
@@ -131,7 +131,6 @@
     pl.semaphore_wait(barrier, (n_ab - 1) + (n_x - 1) + (n_z - 1))
 
     own = pltpu.make_async_copy(packed_ref, slots.at[me_ab], own_sem.at[0])
-    own.start()
     for k in range(1, n_ab):
         peer = lax.rem(me_ab + k, n_ab)
         pltpu.make_async_remote_copy(
@@ -142,6 +141,7 @@
             device_id=(peer, me_cd),
             device_id_type=MESH,
         ).start()
+    own.start()
     for step, owner in enumerate(order):
         pltpu.make_async_copy(
             values_hbm.at[pl.ds(pl.multiple_of(owner * block, block), block), :],

time: 52.1 us -> 52.1 us (level)
  no operation moved by 1% of the time
where the time goes in v19:
time: 52.1 us; the launch traced here: 52 us
  Pallas kernels  41.9 us (80%)
  local copies, waits for them, and re-layouts  7.35 us (14%)
  matrix products  1.8 us (3%)
  between operations  0.8 us (2%)
    pallas_call x1, Pallas kernels, ladder(): pl.pallas_call(functools.partial(ladder_kernel, n_ab, n_x, n_z), out_shap...  26 us
    pallas_call x1, Pallas kernels, exchange(): pl.pallas_call(functools.partial(exchange_kernel, n_cd), out_shape=(jax.S...  16 us
    unnamed x13, local copies, waits for them, and re-layouts  3.28 us
    reshape x1, local copies, waits for them, and re-layouts, on_device(): jnp.transpose(amplitudes, (1, 0, 2))  2.45 us
    dot_general x1, matrix products, on_device(): lax.dot_general(mirrored, pick_d.reshape(n_cd, orbit_block, columns), (((...  1.8 us

profile of v19, /device:TPU:1, one launch (start us, length us, event | category | flops | bytes accessed | tf_op | source)
XLA Modules:
  0.0 52.0 jit_solution(3018247598054496807)
XLA Ops:
  0.0 2.5 %reshape.60 = bf16[50,4,16,50]{3,2,1,0:T(8,128)(2,1)S(1)} reshape(bf16[50,4,800]{2,1,0:T(4,128)(2,1)} %bitcast.30) | data formatting | bytes 640000 | tf_op jit(solution)/shard_map/reshape | solution.py:278
  2.5 0.0 copy-start
  2.5 0.3 copy.8
  2.8 0.5 reshape.61
  3.3 0.8 %copy.12 = bf16[2,8,80,128]{3,2,1,0:T(8,128)(2,1)} copy(bf16[2,8,80,128]{3,1,2,0:T(8,128)(2,1)S(1)} %pad_bitcast_fusion) | data formatting | bytes 655360
  4.1 0.0 copy-done
  4.1 0.0 copy-start.1
  4.1 0.8 %copy.9.amp_ref = bf16[4,50,800]{2,1,0:T(8,128)(2,1)} copy(bf16[4,50,800]{2,0,1:T(4,128)(2,1)S(1)} %copy-done) | data formatting | bytes 640000 | tf_op args[1]
  4.9 0.0 copy-start.2
  4.9 16.0 %shard_map.55 = (bf16[16,80,128]{2,1,0:T(8,128)(2,1)}, f32[4,2048]{1,0:T(4,128)}) custom-call(bf16[16,80,128]{2,1,0:T(8,128)(2,1)} %bitcast.31, bf16[4,50,800]{2,1,0:T(8,128)(2,1)} %copy.9.amp_ref, s32[1,2048]{1,0:T(1,128)} %bitcast.35, s32[1,2048]{1,0:T(1,128)} %bitcast.34), custom_call_target="tpu_custom_call" | custom-call | tf_op jit(solution)/shard_map/pallas_call | solution.py:87
  20.9 1.1 %copy.17 = bf16[2,8,80,128]{3,1,2,0:T(8,128)(2,1)S(1)} copy(bf16[2,8,80,128]{3,2,1,0:T(8,128)(2,1)} %bitcast.33) | data formatting | bytes 655360
  22.0 0.8 %reshape.66 = bf16[16,50,4,50]{3,2,1,0:T(4,128)(2,1)S(1)} reshape(bf16[16,10000]{1,0:T(8,128)(2,1)S(1)} %slice.4) | data formatting | bytes 640000 | tf_op jit(solution)/shard_map/reshape | solution.py:282
  22.8 0.0 copy-done.1
  22.8 0.1 iota_compare_fusion
  22.9 0.0 copy-done.2
  22.9 0.0 copy-start.3
  22.9 1.8 %fusion.11 = f32[4,2048]{1,0:T(4,128)S(1)} fusion(s32[2048]{0:T(1024)S(1)} %copy-done.2, s32[16,50]{1,0:T(8,128)S(1)} %multiply_add_fusion, bf16[16,50,4,50]{3,2,1,0:T(4,128)(2,1)S(1)} %reshape.66, pred[50,2048]{1,0:T(8,128)(4,1)S(1)} %iota_compare_fusion), kind=kOutput, calls=%fused_computation.7 | convolution fusion | flops 657809408 | bytes 466560 | tf_op jit(solution)/shard_map/dot_general | solution.py:286
  25.4 0.0 copy-done.3
  25.4 26.0 %shard_map.56 = bf16[64,128]{1,0:T(8,128)(2,1)S(1)} custom-call(bf16[4,2048]{1,0:T(4,128)(2,1)S(1)} %multiply_convert_fusion.packed_ref, bf16[2048,2048]{1,0:T(8,128)(2,1)} %values_hbm.1), custom_call_target="tpu_custom_call" | custom-call | tf_op jit(solution)/shard_map/pallas_call | solution.py:241
  51.4 0.6 %copy.20 = bf16[64,128]{1,0:T(8,128)(2,1)} copy(bf16[64,128]{1,0:T(8,128)(2,1)S(1)} %shard_map.56) | data formatting | bytes 32768
  (6 shorter events, 0.1 us)
Async XLA Ops:
  2.5 1.6 %copy-start = (bf16[4,50,800]{2,0,1:T(4,128)(2,1)S(1)}, bf16[4,50,800]{2,0,1:T(4,128)(2,1)}, u32[]{:S(2)}) copy-start(bf16[4,50,800]{2,0,1:T(4,128)(2,1)} %param.6) | copy-start | bytes 960004
  4.1 18.7 %copy-start.1 = (s32[2048]{0:T(1024)S(1)}, s32[2048]{0:T(1024)}, u32[]{:S(2)}) copy-start(s32[2048]{0:T(1024)} %param.7) | copy-start | bytes 24580
  4.9 18.0 %copy-start.2 = (s32[2048]{0:T(1024)S(1)}, s32[2048]{0:T(1024)}, u32[]{:S(2)}) copy-start(s32[2048]{0:T(1024)} %param.8) | copy-start | bytes 24580
  22.9 2.5 %copy-start.3 = (f32[4,2048]{1,0:T(4,128)S(1)}, f32[4,2048]{1,0:T(4,128)}, u32[]{:S(2)}) copy-start(f32[4,2048]{1,0:T(4,128)} %get-tuple-element.7) | copy-start | bytes 98308
